TPU v7x, 512 devices: a whole 4x8x8 slice. The times are simulated.
512 devices in a mesh: wide: 64 (over z, y_hi, core), narrow: 8 (over x, y_lo).
Axes of the slice: x: 4, y: 8 (y_hi: 4, y_lo: 2; y = y_hi * 2 + y_lo), z: 8, core: 2. Of those that a mesh axis runs over, the one named last changes fastest.
Arguments:
- hidden_in: bfloat16 [16384, 2048], P('wide', 'narrow'), may hold values from -64 to 64
- cache_lengths: int32 [128], P('wide'), may hold values from 1 to 1023, as said below
- cache_offsets: int32 [128], P('wide'), may hold values from 0 to 65535, as said below
- cache_kv: bfloat16 [2, 2, 65536, 2048], P(None, None, 'wide', 'narrow'), may hold values from -16 to 16
- w_qkv: bfloat16 [2048, 3, 2048], P('wide', None, 'narrow'), may hold values from -0.125 to 0.125
- qkv_bias: bfloat16 [3, 2048], P(None, 'narrow'), may hold values from -40 to 40
- w_out: bfloat16 [2048, 2048], P('wide', 'narrow'), may hold values from -0.125 to 0.125
- out_bias: bfloat16 [2048], P('narrow'), may hold values from -3 to 3
- norm_gain: bfloat16 [2048], P('narrow'), may hold values from 0.2 to 5
- norm_shift: bfloat16 [2048], P('narrow'), may hold values from -3 to 3
Outputs:
- hidden_out: bfloat16 [16384, 2048], P('wide', 'narrow')
- new_cache: bfloat16 [2, 2, 16384, 2048], P(None, None, 'wide', 'narrow')
Inputs may be any that keep to these rules, and one draw needn't show every extreme that they name: `cache_lengths`: the cached lengths of the 2 requests r with the same r // 2 sum to at most 1024; for some such group exactly 1024, and in it one request has 1023 rows. Request r's cache is rows cache_offsets[r] to cache_offsets[r] + cache_lengths[r] - 1 of the packed cache, all within rows (r // 2) * 1024 to (r // 2 + 1) * 1024 - 1; the row ranges of different requests are disjoint.
All inputs are finite; a program needn't handle non-finite values.
Results may differ from a plain program's by a relative error of at most 0.02.
Values may be sent and summed in bfloat16 or wider, within the bound.
No kernel may reach another device: no remote copies, remote signals or barrier semaphores. Data moves between devices by JAX's collectives and lax.ppermute only.
A program may use at most 64 MiB of HBM per device.

v0:
```python
import math

import jax
import jax.numpy as jnp
from jax import lax
from jax.sharding import PartitionSpec as P

HEAD = 128
SPAN = 128
LAYERS = 2


EPSILON = 1e-05
NEGATIVE = -1e30


def add_rows(shard_piece, operand):
    piece_rows = shard_piece.shape[0]
    return jnp.dot(operand, shard_piece.reshape(piece_rows, -1), preferred_element_type=jnp.float32)


def norm_slice(summed, norm_gain, norm_shift, full_width):
    values = summed.astype(jnp.float32)
    row_means = lax.psum(jnp.sum(values, axis=1), "narrow") / full_width
    centered = values - row_means[:, None]
    row_spread = lax.psum(jnp.sum(centered * centered, axis=1), "narrow") / full_width
    scaled = centered * lax.rsqrt(row_spread[:, None] + EPSILON)
    return (scaled * norm_gain.astype(jnp.float32) + norm_shift.astype(jnp.float32)).astype(
        jnp.bfloat16
    )


def attend(queries, keys_new, values_new, keys_cache, values_cache, live_cache, live_new):
    scale_factor = 1.0 / math.sqrt(queries.shape[2])
    scores_cache = (
        jnp.einsum("qhd,khd->hqk", queries, keys_cache, preferred_element_type=jnp.float32)
        * scale_factor
    )
    scores_new = (
        jnp.einsum("qhd,khd->hqk", queries, keys_new, preferred_element_type=jnp.float32)
        * scale_factor
    )
    masked_cache = jnp.where(live_cache[None], scores_cache, NEGATIVE)
    masked_new = jnp.where(live_new[None], scores_new, NEGATIVE)
    top_score = jnp.maximum(jnp.max(masked_cache, axis=2), jnp.max(masked_new, axis=2))[:, :, None]
    weights_cache = jnp.where(live_cache[None], jnp.exp(masked_cache - top_score), 0.0)
    weights_new = jnp.where(live_new[None], jnp.exp(masked_new - top_score), 0.0)
    totals = jnp.sum(weights_cache, axis=2, keepdims=True) + jnp.sum(
        weights_new, axis=2, keepdims=True
    )
    probs_cache = (weights_cache / totals).astype(jnp.bfloat16)
    probs_new = (weights_new / totals).astype(jnp.bfloat16)
    combined = jnp.einsum(
        "hqk,khd->qhd", probs_cache, values_cache, preferred_element_type=jnp.float32
    )
    combined = combined + jnp.einsum(
        "hqk,khd->qhd", probs_new, values_new, preferred_element_type=jnp.float32
    )
    return combined.astype(jnp.bfloat16).reshape(queries.shape[0], -1)


def shards(
    hidden_in,
    cache_lengths,
    cache_offsets,
    cache_kv,
    w_qkv,
    qkv_bias,
    w_out,
    out_bias,
    norm_gain,
    norm_shift,
):
    row_count, local_width = hidden_in.shape
    full_width = local_width * lax.axis_size("narrow")
    local_heads = local_width // HEAD
    cache_count = cache_kv.shape[2]
    requests_here = cache_lengths.shape[0]
    block_start = lax.axis_index("wide") * cache_count
    rows_global = block_start + jnp.arange(cache_count, dtype=jnp.int32)
    row_start = jnp.broadcast_to(cache_offsets[:, None], (requests_here, SPAN)).reshape(-1)
    row_stop = row_start + jnp.broadcast_to(cache_lengths[:, None], (requests_here, SPAN)).reshape(
        -1
    )
    live_cache = (rows_global[None, :] >= row_start[:, None]) & (
        rows_global[None, :] < row_stop[:, None]
    )
    owner_index = jnp.arange(row_count, dtype=jnp.int32) // SPAN
    position = jnp.arange(row_count, dtype=jnp.int32) % SPAN
    live_new = (owner_index[:, None] == owner_index[None, :]) & (
        position[:, None] >= position[None, :]
    )
    bias_flat = qkv_bias.astype(jnp.float32).reshape(-1)
    gathered = lax.all_gather(hidden_in, "narrow", axis=1, tiled=True)
    carried = hidden_in
    appended = []
    for layer_index in range(LAYERS):
        projections = add_rows(lax.all_gather(w_qkv, "wide", axis=0, tiled=True), operand=gathered)
        projections = projections + bias_flat
        queries = projections[:, :local_width].astype(jnp.bfloat16)
        keys_new = projections[:, local_width : 2 * local_width].astype(jnp.bfloat16)
        values_new = projections[:, 2 * local_width :].astype(jnp.bfloat16)
        appended.append(jnp.stack([keys_new, values_new]))
        keys_cache = cache_kv[layer_index, 0].reshape(cache_count, local_heads, HEAD)
        values_cache = cache_kv[layer_index, 1].reshape(cache_count, local_heads, HEAD)
        attended = attend(
            queries.reshape(row_count, local_heads, HEAD),
            keys_new.reshape(row_count, local_heads, HEAD),
            values_new.reshape(row_count, local_heads, HEAD),
            keys_cache,
            values_cache,
            live_cache,
            live_new,
        )
        heads_all = lax.all_gather(attended, "narrow", axis=1, tiled=True)
        projected = add_rows(lax.all_gather(w_out, "wide", axis=0, tiled=True), operand=heads_all)
        summed = (projected + out_bias.astype(jnp.float32) + carried.astype(jnp.float32)).astype(
            jnp.bfloat16
        )
        if layer_index + 1 < LAYERS:
            carried = norm_slice(summed, norm_gain, norm_shift, full_width)
            gathered = lax.all_gather(carried, "narrow", axis=1, tiled=True)
        else:
            carried = norm_slice(summed, norm_gain, norm_shift, full_width)
    return (carried, jnp.stack(appended))


def solution(mesh):
    in_specs = (
        P("wide", "narrow"),
        P("wide"),
        P("wide"),
        P(None, None, "wide", "narrow"),
        P("wide", None, "narrow"),
        P(None, "narrow"),
        P("wide", "narrow"),
        P("narrow"),
        P("narrow"),
        P("narrow"),
    )
    out_specs = (P("wide", "narrow"), P(None, None, "wide", "narrow"))
    return jax.shard_map(shards, mesh=mesh, in_specs=in_specs, out_specs=out_specs, check_vma=False)
```

profile of v0, /device:TPU:56, one launch (start us, length us, event | category | flops | bytes accessed | tf_op | source)
XLA Modules:
  0.0 457.3 jit_solution(16025079761975126802)
XLA Ops:
  11.6 2.6 fusion.54
  16.7 84.3 %all-gather.9.cloned.1.call-done = bf16[2048,3,256]{2,0,1:T(8,128)(2,1)} async-done(((bf16[32,3,256]{2,0,1:T(8,128)(2,1)}), bf16[2048,3,256]{2,0,1:T(8,128)(2,1)}) %all-gather.9.cloned.1.call-update) | async-done | bytes 3145744 | tf_op jit(solution)/shard_map/all_gather | solution.py:98
  101.0 3.2 copy.45
  104.2 40.3 %all-gather.7.cloned.1.call-done = bf16[256,2048]{1,0:T(8,128)(2,1)} async-done(((bf16[256,256]{1,0:T(8,128)(2,1)}), bf16[256,2048]{1,0:T(8,128)(2,1)}) %all-gather.7.cloned.1.call-update) | async-done | bytes 1048592 | tf_op jit(solution)/shard_map/all_gather | solution.py:94
  144.5 2.2 fusion.4
  147.6 1.7 copy.68
  149.2 1.2 fusion.55
  150.4 1.8 fusion
  155.2 1.7 copy.54
  156.9 73.9 %all-gather.13.cloned.1.call-done = bf16[2048,256]{1,0:T(8,128)(2,1)} async-done(((bf16[32,256]{1,0:T(8,128)(2,1)}), bf16[2048,256]{1,0:T(8,128)(2,1)}) %all-gather.13.cloned.1.call-update) | async-done | bytes 1048592 | tf_op jit(solution)/shard_map/all_gather | solution.py:116
  230.8 43.4 %all-gather.11.cloned.1.call-done = bf16[256,2048]{0,1:T(8,128)(2,1)} async-done(((bf16[256,256]{0,1:T(8,128)(2,1)}), bf16[256,2048]{0,1:T(8,128)(2,1)}) %all-gather.11.cloned.1.call-update) | async-done | bytes 1048592 | tf_op jit(solution)/shard_map/all_gather | solution.py:115
  274.2 2.8 fusion.56
  277.0 18.7 %psum.28 = f32[256]{0:T(256)S(1)} all-reduce(f32[256]{0:T(256)S(1)} %get-tuple-element.26), channel_id=1, replica_groups=mesh['wide'=64,'narrow'=8] {'narrow'}, use_global_device_ids=true, to_apply=%region_5.6 | all-reduce | flops 256 | bytes 2048 | tf_op jit(solution)/shard_map/psum | solution.py:24
  296.7 17.6 %psum.29 = f32[256]{0:T(256)S(1)} all-reduce(f32[256]{0:T(256)S(1)} %multiply_reduce_fusion.1), channel_id=1, replica_groups=mesh['wide'=64,'narrow'=8] {'narrow'}, use_global_device_ids=true, to_apply=%region_7.8 | all-reduce | flops 256 | bytes 2048 | tf_op jit(solution)/shard_map/psum | solution.py:26
  314.3 1.7 add_convert_fusion.1
  316.1 2.0 copy.71
  318.1 2.0 copy.60
  320.2 37.9 %all-gather.15.cloned.1.call-done = bf16[256,2048]{0,1:T(8,128)(2,1)} async-done(((bf16[256,256]{0,1:T(8,128)(2,1)}), bf16[256,2048]{0,1:T(8,128)(2,1)}) %all-gather.15.cloned.1.call-update) | async-done | bytes 1048592 | tf_op jit(solution)/shard_map/all_gather | solution.py:122
  358.0 2.3 fusion.5
  363.0 1.7 copy.69
  367.5 43.9 %all-gather.17.cloned.1.call-done = bf16[256,2048]{0,1:T(8,128)(2,1)} async-done(((bf16[256,256]{0,1:T(8,128)(2,1)}), bf16[256,2048]{0,1:T(8,128)(2,1)}) %all-gather.17.cloned.1.call-update) | async-done | bytes 1048592 | tf_op jit(solution)/shard_map/all_gather | solution.py:115
  411.4 1.8 fusion.58
  413.2 18.7 %psum.30 = f32[256]{0:T(256)S(1)} all-reduce(f32[256]{0:T(256)S(1)} %get-tuple-element.32), channel_id=1, replica_groups=mesh['wide'=64,'narrow'=8] {'narrow'}, use_global_device_ids=true, to_apply=%region_13.14 | all-reduce | flops 256 | bytes 2048 | tf_op jit(solution)/shard_map/psum | solution.py:24
  432.0 17.6 %psum.31 = f32[256]{0:T(256)S(1)} all-reduce(f32[256]{0:T(256)S(1)} %multiply_reduce_fusion), channel_id=1, replica_groups=mesh['wide'=64,'narrow'=8] {'narrow'}, use_global_device_ids=true, to_apply=%region_15.16 | all-reduce | flops 256 | bytes 2048 | tf_op jit(solution)/shard_map/psum | solution.py:26
  (79 shorter events, 18.0 us)
Async XLA Ops:
  7.2 93.8 %all-gather.9.cloned.1.call-start = ((), (), s32[]{:S(2)}) async-start(), calls=%async_computation.1 | async-start | bytes 3194880 | tf_op jit(solution)/shard_map/all_gather | solution.py:98
  7.9 136.6 %all-gather.7.cloned.1.call-start = ((), (), s32[]{:S(2)}) async-start(), calls=%async_computation | async-start | bytes 1179648 | tf_op jit(solution)/shard_map/all_gather | solution.py:94
  8.6 222.2 %all-gather.13.cloned.1.call-start = ((), (), s32[]{:S(2)}) async-start(), calls=%async_computation.3 | async-start | bytes 1064960 | tf_op jit(solution)/shard_map/all_gather | solution.py:116
  9.4 264.8 %all-gather.11.cloned.1.call-start = ((), (), s32[]{:S(2)}) async-start(), calls=%async_computation.2 | async-start | bytes 1179648 | tf_op jit(solution)/shard_map/all_gather | solution.py:115
  152.2 1.0 copy-start.2
  153.2 0.9 copy-start.8
  154.1 2.7 copy-start.11
  154.1 2.7 copy-start.12
  154.1 2.7 copy-start.13
  155.1 202.9 %all-gather.15.cloned.1.call-start = ((), (), s32[]{:S(2)}) async-start(), calls=%async_computation.4 | async-start | bytes 1179648 | tf_op jit(solution)/shard_map/all_gather | solution.py:122
  316.0 95.3 %all-gather.17.cloned.1.call-start = ((), (), s32[]{:S(2)}) async-start(), calls=%async_computation.5 | async-start | bytes 1179648 | tf_op jit(solution)/shard_map/all_gather | solution.py:115
  358.0 3.4 copy-start
  362.0 2.6 copy-start.3
  364.7 0.9 copy-start.9
  365.5 1.0 copy-start.4
  365.5 1.0 copy-start.5
  365.5 1.1 copy-start.6
  365.5 1.1 copy-start.7
  365.6 45.8 %copy-start.1 = (bf16[256,256]{0,1:T(8,128)(2,1)S(1)}, bf16[256,256]{0,1:T(8,128)(2,1)}, u32[]{:S(2)}) copy-start(bf16[256,256]{0,1:T(8,128)(2,1)} %add_convert_fusion.1) | copy-start | bytes 393220
  365.6 45.8 %copy-start.10 = (bf16[2048,256]{1,0:T(8,128)(2,1)S(1)}, bf16[2048,256]{1,0:T(8,128)(2,1)}, u32[]{:S(2)}) copy-start(bf16[2048,256]{1,0:T(8,128)(2,1)} %all-gather.13.cloned.1.call-done) | copy-start | bytes 3145732
Sparse Core Ops, SparseCore 0:
  11.4 89.5 all-gather.8
  103.0 41.4 all-gather.6
  147.8 82.9 all-gather.12
  232.7 41.4 all-gather.10
  316.2 41.8 all-gather.14
  366.6 44.6 all-gather.16
where the time goes:
time: 458 us; the launch traced here: 457 us
  waiting for transfers between devices  326 us (71%)
  blocking collectives  72.6 us (16%)
  local copies, waits for them, and re-layouts  20.9 us (5%)
  matrix products  16.5 us (4%)
  between operations  14.4 us (3%)
  other arithmetic  6.96 us (2%)
    all_gather x2, waiting for transfers between devices, shards(): heads_all = lax.all_gather(attended, 'narrow', axis=1, tiled=True)  87.3 us
    all_gather x1, waiting for transfers between devices, shards(): lax.all_gather(w_qkv, 'wide', axis=0, tiled=True)  84.3 us
    all_gather x1, waiting for transfers between devices, shards(): lax.all_gather(w_out, 'wide', axis=0, tiled=True)  73.9 us
    all_gather x1, waiting for transfers between devices, shards(): gathered = lax.all_gather(hidden_in, 'narrow', axis=1, tiled=True)  40.3 us
    all_gather x1, waiting for transfers between devices, shards(): gathered = lax.all_gather(carried, 'narrow', axis=1, tiled=True)  37.9 us
    psum x2, blocking collectives, norm_slice(): row_means = lax.psum(jnp.sum(values, axis=1), 'narrow') / full_width  37.4 us
    psum x2, blocking collectives, norm_slice(): lax.psum(jnp.sum(centered * centered, axis=1), 'narrow') / full_width  35.2 us
  transfers between devices with their start and end apart: 6, of which 6 were waited for; matrix products, arithmetic and copies ran while one was open for 6% of the time, Pallas kernels for 0%

commit v1 on v0

v1 whole, which is shorter than its diff:
```python
import functools
import math

import jax
import jax.numpy as jnp
from jax import lax
from jax.experimental import pallas as pl
from jax.experimental.pallas import tpu as pltpu
from jax.sharding import Mesh
from jax.sharding import PartitionSpec as P

HEAD = 128
SPAN = 128
EPSILON = 1e-05
NEGATIVE = -1e30
AXES = ("z", "yh", "c", "x", "yl")
SIZES = (8, 4, 2, 4, 2)
WIDE = ("z", "yh", "c")
NARROW = ("x", "yl")
SWAP = [(0, 1), (1, 0)]
VMEM_LIMIT = 40 * 1024 * 1024
F32 = jnp.float32
BF16 = jnp.bfloat16


def spread(x, axes, count):
    return lax.all_to_all(jnp.broadcast_to(x[None], (count,) + x.shape), axes, 0, 0, tiled=True)


def dot(a, b):
    return jnp.dot(a, b, preferred_element_type=F32)


def dot_t(a, b):
    return lax.dot_general(a, b, (((1,), (1,)), ((), ())), preferred_element_type=F32)


def rows_of(own, other, low, z, j):
    parts = []
    for y in range(4):
        mine, theirs = own[z, y, j], other[z, y, j]
        parts += [jnp.where(low, mine, theirs), jnp.where(low, theirs, mine)]
    return jnp.concatenate(parts, axis=0)


def attention_kernel(
    first, info, starts, stops, x_ref, gs_ref, bias_ref, cache, prev, own, other, *rest
):
    if first:
        att_ref, new_ref = rest
        x = x_ref
    else:
        att_ref, new_ref, res_ref, x = rest
        total = jnp.zeros((256, 1), F32)
        for n in range(8):
            total += jnp.sum(x_ref[n, 0:256, :].astype(F32), axis=1, keepdims=True)
        mean = total / 2048.0
        spread_sum = jnp.zeros((256, 1), F32)
        for n in range(8):
            centered = x_ref[n, 0:256, :].astype(F32) - mean
            spread_sum += jnp.sum(centered * centered, axis=1, keepdims=True)
        scale = lax.rsqrt(spread_sum / 2048.0 + EPSILON)
        for n in range(8):
            both = gs_ref[n].astype(F32)
            gain = both[0:1]
            shift = both[1:2]
            x[n] = ((x_ref[n, 0:256, :].astype(F32) - mean) * scale * gain + shift).astype(BF16)
        res_ref[...] = x[info[1]]
    low = info[0] == 0
    bias = bias_ref[...]
    parts = []
    for j in range(3):
        acc = dot(x[0, 0:256, :], rows_of(own, other, low, 0, j))
        for n in range(1, 8):
            acc += dot(x[n, 0:256, :], rows_of(own, other, low, n, j))
        parts.append((acc + bias[j : j + 1]).astype(BF16))
    q, k_new, v_new = parts
    new_ref[0, 0] = k_new
    new_ref[0, 1] = v_new
    factor = 1.0 / math.sqrt(HEAD)
    column = lax.broadcasted_iota(jnp.int32, (1, 1024), 1)
    causal = lax.broadcasted_iota(jnp.int32, (SPAN, SPAN), 0) >= lax.broadcasted_iota(
        jnp.int32, (SPAN, SPAN), 1
    )
    for r in range(2):
        rows = slice(r * SPAN, (r + 1) * SPAN)
        live = (column >= starts[r]) & (column < stops[r])
        for h in range(2):
            cols = slice(h * HEAD, (h + 1) * HEAD)
            qh = q[rows, cols]
            sc = jnp.where(live, dot_t(qh, cache[0, 0, :, cols]) * factor, NEGATIVE)
            sn = jnp.where(causal, dot_t(qh, k_new[rows, cols]) * factor, NEGATIVE)
            top = jnp.maximum(
                jnp.max(sc, axis=1, keepdims=True), jnp.max(sn, axis=1, keepdims=True)
            )
            pc = jnp.exp(sc - top)
            pn = jnp.exp(sn - top)
            norm = jnp.sum(pc, axis=1, keepdims=True) + jnp.sum(pn, axis=1, keepdims=True)
            out = dot(pc.astype(BF16), cache[0, 1, :, cols]) + dot(
                pn.astype(BF16), v_new[rows, cols]
            )
            att_ref[rows, cols] = (out / norm).astype(BF16)


def piece_specs(j, count):
    return [pl.BlockSpec((8, 4, count, 32, 256), lambda i: (0, 0, j, 0, 0))] * 2


def attention(first, layer, info, starts, stops, x, gathered, bias, cache, prev, pieces):
    smem = pl.BlockSpec(memory_space=pltpu.SMEM)

    def whole(a):
        return pl.BlockSpec(a.shape, lambda i: (0,) * a.ndim)

    rows = x.shape[1]
    in_specs = [
        smem,
        smem,
        smem,
        pl.BlockSpec((8, rows, 256), lambda i: (0, 0, 0)),
        pl.BlockSpec((8, 16, 256), lambda i: (0, 0 if first else 16, 0)),
        whole(bias),
        pl.BlockSpec((1, 2, 1024, 256), lambda i: (layer, 0, 0, 0)),
        pl.BlockSpec(memory_space=pl.ANY),
    ] + piece_specs(0, 3)
    tile = jax.ShapeDtypeStruct((256, 256), BF16)
    out_shape = [tile, jax.ShapeDtypeStruct((2, 2, 256, 256), BF16)]
    tile_spec = pl.BlockSpec((256, 256), lambda i: (0, 0))
    out_specs = [tile_spec, pl.BlockSpec((1, 2, 256, 256), lambda i: (layer, 0, 0, 0))]
    scratch = []
    aliases = {}
    if not first:
        out_shape.append(tile)
        out_specs.append(tile_spec)
        scratch.append(pltpu.VMEM((8, 256, 256), BF16))
        aliases = {7: 1}
    return pl.pallas_call(
        functools.partial(attention_kernel, first),
        grid=(1,),
        out_shape=out_shape,
        in_specs=in_specs,
        out_specs=out_specs,
        scratch_shapes=scratch,
        input_output_aliases=aliases,
        compiler_params=pltpu.CompilerParams(vmem_limit_bytes=VMEM_LIMIT),
        cost_estimate=pl.CostEstimate(
            flops=2 * 256 * 2048 * 768 + 4 * 256 * 1152 * 256,
            bytes_accessed=6 << 20,
            transcendentals=256 * 1152 * 2,
        ),
        name="attention",
    )(info, starts, stops, x, gathered, bias, cache, prev, *pieces)


def project_kernel(last, info, att, bias_ref, res_ref, gs_ref, own, other, *rest):
    out_ref = rest[0]
    low = info[0] == 0
    acc = dot(att[0], rows_of(own, other, low, 0, 0))
    for n in range(1, 8):
        acc += dot(att[n], rows_of(own, other, low, n, 0))
    summed = (acc + bias_ref[0:1, :] + res_ref[...].astype(F32)).astype(BF16)
    out_ref[0:256, :] = summed
    if last:
        values = summed.astype(F32)
        mean = jnp.sum(values, axis=1, keepdims=True) / 256.0
        centered = values - mean
        spread_sum = jnp.sum(centered * centered, axis=1, keepdims=True)
        lane = lax.broadcasted_iota(jnp.int32, (256, 128), 1)
        stats = jnp.where(lane == 0, mean, spread_sum)
        rest[1][...] = stats.T[0:8, :]
    else:
        out_ref[256:272, :] = gs_ref[...]


def project(last, info, att, bias, res, gs, pieces):
    def whole(a):
        return pl.BlockSpec(a.shape, lambda i: (0,) * a.ndim)

    out_shape = [jax.ShapeDtypeStruct((256 if last else 272, 256), BF16)]
    if last:
        out_shape.append(jax.ShapeDtypeStruct((8, 256), F32))
    return pl.pallas_call(
        functools.partial(project_kernel, last),
        grid=(1,),
        out_shape=out_shape,
        in_specs=[pl.BlockSpec(memory_space=pltpu.SMEM)]
        + [whole(a) for a in (att, bias, res, gs)]
        + piece_specs(3, 1),
        out_specs=[whole(a) for a in out_shape],
        compiler_params=pltpu.CompilerParams(vmem_limit_bytes=VMEM_LIMIT),
        cost_estimate=pl.CostEstimate(
            flops=2 * 256 * 2048 * 256, bytes_accessed=3 << 20, transcendentals=0
        ),
        name="project",
    )(info, att, bias, res, gs, *pieces)


def finish_kernel(stats, summed, gain_ref, shift_ref, out_ref):
    means = [stats[n, 0:1, :] for n in range(8)]
    mean = functools.reduce(lambda a, b: a + b, means) / 8.0
    total = jnp.zeros((1, 256), F32)
    for n in range(8):
        offset = means[n] - mean
        total += stats[n, 1:2, :] + 256.0 * offset * offset
    scale = lax.rsqrt(total / 2048.0 + EPSILON)
    row = lax.broadcasted_iota(jnp.int32, (128, 256), 0)
    columns = jnp.where(row == 0, mean, scale).T
    values = summed[...].astype(F32)
    scaled = (values - columns[:, 0:1]) * columns[:, 1:2]
    out_ref[...] = (scaled * gain_ref[...].astype(F32) + shift_ref[...].astype(F32)).astype(BF16)


def finish(stats, summed, gain, shift):
    return pl.pallas_call(
        finish_kernel,
        out_shape=jax.ShapeDtypeStruct((256, 256), BF16),
        name="finish",
    )(stats, summed, gain, shift)


def shards(
    hidden_in,
    cache_lengths,
    cache_offsets,
    cache_kv,
    w_qkv,
    qkv_bias,
    w_out,
    out_bias,
    norm_gain,
    norm_shift,
):
    cache_count = cache_kv.shape[2]
    info = jnp.stack([lax.axis_index("c"), lax.axis_index(NARROW), lax.axis_index("yh")])
    starts = cache_offsets - lax.axis_index(WIDE) * cache_count
    stops = starts + cache_lengths
    gs = jnp.concatenate([norm_gain[None], norm_shift[None], jnp.zeros((14, 256), BF16)], axis=0)
    bias = jnp.pad(qkv_bias.astype(F32), ((0, 5), (0, 0)))
    out_b = jnp.broadcast_to(out_bias.astype(F32)[None], (8, 256))
    gain = norm_gain.reshape(1, -1)
    shift = norm_shift.reshape(1, -1)

    pieces = jnp.concatenate([w_qkv.transpose(1, 0, 2), w_out[None]], axis=0)
    near = spread(pieces, "yh", 4)
    near, entry = lax.optimization_barrier((near, hidden_in))
    own = lax.all_gather(near.reshape(512, 256), "z", axis=0, tiled=True)
    gathered = spread(entry, NARROW, 8)
    own, gathered = lax.optimization_barrier((own, gathered))
    other = lax.ppermute(own, "c", SWAP)
    pieces = [own.reshape(8, 4, 4, 32, 256), other.reshape(8, 4, 4, 32, 256)]

    blank = jnp.zeros((8, 128), BF16)
    att, new_cache = attention(
        True, 0, info, starts, stops, gathered, gathered, bias, cache_kv, blank, pieces
    )
    heads = spread(att, NARROW, 8)
    (summed,) = project(False, info, heads, out_b, hidden_in, gs, pieces)
    rows = spread(summed, NARROW, 8)
    att, new_cache, carried = attention(
        False, 1, info, starts, stops, rows, rows, bias, cache_kv, new_cache, pieces
    )
    heads = spread(att, NARROW, 8)
    summed, stats = project(True, info, heads, out_b, carried, gs, pieces)
    hidden_out = finish(spread(stats, NARROW, 8), summed, gain, shift)
    return hidden_out, new_cache


def solution(mesh):
    split = Mesh(mesh.devices.reshape(SIZES), AXES)
    in_specs = (
        P(WIDE, NARROW),
        P(WIDE),
        P(WIDE),
        P(None, None, WIDE, NARROW),
        P(WIDE, None, NARROW),
        P(None, NARROW),
        P(WIDE, NARROW),
        P(NARROW),
        P(NARROW),
        P(NARROW),
    )
    out_specs = (P(WIDE, NARROW), P(None, None, WIDE, NARROW))
    return jax.shard_map(shards, mesh=split, in_specs=in_specs, out_specs=out_specs, check_vma=False)
```

time: 458 us -> 172 us (0.38)
  waiting for transfers between devices: 326 us -> 46.3 us
  matrix products: 16.5 us -> 0 us
  local copies, waits for them, and re-layouts: 20.9 us -> 9.09 us
  Pallas kernels: 0 us -> 11.6 us
  blocking collectives: 72.6 us -> 80.2 us
  starting transfers between devices: 0.24 us -> 7.66 us
  other arithmetic: 6.96 us -> 0.99 us
    all_gather x6 -> x1, waiting for transfers between devices: 324 us -> 27.4 us  [shards(): own = lax.all_gather(near.reshape(512, 256), 'z', axis=0, tiled=True)]
    all_to_all x0 -> x5, blocking collectives: none -> 80.2 us  [spread(): lax.all_to_all(jnp.broadcast_to(x[None], (count,) + x.shape), axes, 0, 0,...]
    psum x4 -> x0, blocking collectives: 72.6 us -> none  [the longest x2 37.4 us: norm_slice(): row_means = lax.psum(jnp.sum(values, axis=1), 'narrow') / full_width]
    dot_general x12 -> x0, matrix products: 16.5 us -> none  [the longest x4 9.16 us: add_rows(): jnp.dot(operand, shard_piece.reshape(piece_rows, -1), preferred_element_t...]
    all_to_all x0 -> x1, waiting for transfers between devices: none -> 14.6 us  [spread(): lax.all_to_all(jnp.broadcast_to(x[None], (count,) + x.shape), axes, 0, 0,...]
    pallas_call x0 -> x5, Pallas kernels: none -> 11.6 us  [the longest x2 7.62 us: attention(): pl.pallas_call(functools.partial(attention_kernel, first), grid=(1,), out...]
    all_to_all x0 -> x1, starting transfers between devices: none -> 5.71 us  [spread(): lax.all_to_all(jnp.broadcast_to(x[None], (count,) + x.shape), axes, 0, 0,...]
    slice x3 -> x0, local copies, waits for them, and re-layouts: 5.69 us -> none  [the longest x2 3.06 us: shards(): cache_kv[layer_index, 1].reshape(cache_count, local_heads, HEAD)]
  transfers between devices with their start and end apart: 6 -> 3, of which waited for: 6 -> 3; matrix products, arithmetic and copies ran while one was open for 6% -> 1% of each run, Pallas kernels for 0% -> 0%
where the time goes in v1:
time: 172 us; the launch traced here: 170 us
  blocking collectives  80.2 us (47%)
  waiting for transfers between devices  46.3 us (27%)
  between operations  14.3 us (8%)
  Pallas kernels  11.6 us (7%)
  local copies, waits for them, and re-layouts  9.09 us (5%)
  starting transfers between devices  7.66 us (4%)
    all_to_all x5, blocking collectives, spread(): lax.all_to_all(jnp.broadcast_to(x[None], (count,) + x.shape), axes, 0, 0,...  80.2 us
    all_gather x1, waiting for transfers between devices, shards(): own = lax.all_gather(near.reshape(512, 256), 'z', axis=0, tiled=True)  27.4 us
    all_to_all x1, waiting for transfers between devices, spread(): lax.all_to_all(jnp.broadcast_to(x[None], (count,) + x.shape), axes, 0, 0,...  14.6 us
    pallas_call x2, Pallas kernels, attention(): pl.pallas_call(functools.partial(attention_kernel, first), grid=(1,), out...  7.62 us
    unnamed x34, local copies, waits for them, and re-layouts  6.78 us
    all_to_all x1, starting transfers between devices, spread(): lax.all_to_all(jnp.broadcast_to(x[None], (count,) + x.shape), axes, 0, 0,...  5.71 us
    ppermute x1, waiting for transfers between devices, shards(): other = lax.ppermute(own, 'c', SWAP)  4.21 us
  transfers between devices with their start and end apart: 3, of which 3 were waited for; matrix products, arithmetic and copies ran while one was open for 1% of the time, Pallas kernels for 0%

profile of v1, /device:TPU:56, one launch (start us, length us, event | category | flops | bytes accessed | tf_op | source)
XLA Modules:
  0.0 170.1 jit_solution(9818230861818027667)
XLA Ops:
  7.2 0.8 pad_maximum_fusion
  8.1 12.6 %all_to_all.30 = bf16[4,4,32,256]{3,2,1,0:T(8,128)(2,1)} all-to-all(bf16[4,4,32,256]{3,2,1,0:T(8,128)(2,1)S(1)} %broadcast_in_dim.25), channel_id=1, replica_groups=mesh['z'=8,'yh'=4,'c'=2,'x'=4,'yl'=2] {'yh'}, dimensions={0} | all-to-all | bytes 524288 | tf_op jit(solution)/shard_map/all_to_all | solution.py:27
  20.7 1.0 broadcast_in_dim.26
  21.7 21.6 %all_to_all.31.x_ref.gs_ref = bf16[8,256,256]{2,1,0:T(8,128)(2,1)S(1)} all-to-all(bf16[8,256,256]{2,1,0:T(8,128)(2,1)S(1)} %broadcast_in_dim.26), channel_id=1, replica_groups=mesh['z'=8,'yh'=4,'c'=2,'x'=4,'yl'=2] {'x','yl'}, dimensions={0} | all-to-all | bytes 2097152 | tf_op jit(solution)/shard_map/all_to_all | solution.py:27
  43.3 27.4 %all-gather.2.cloned.1.call-done = bf16[4096,256]{1,0:T(8,128)(2,1)} async-done(((bf16[512,256]{1,0:T(8,128)(2,1)}), bf16[4096,256]{1,0:T(8,128)(2,1)}) %all-gather.2.cloned.1.call-update) | async-done | bytes 2097168 | tf_op jit(solution)/shard_map/all_gather | solution.py:246
  70.7 1.9 %collective-permute-start = (bf16[4096,256]{1,0:T(8,128)(2,1)}, bf16[4096,256]{1,0:T(8,128)(2,1)S(1)}, u32[]{:S(2)}, u32[]{:S(2)}) collective-permute-start(bf16[4096,256]{1,0:T(8,128)(2,1)} %all-gather.2.cloned.1.call-done), channel_id=1, source_target_pairs={{0,8},{8,0},{1,9},{9,1},{2,10},{10,2},{3,11},{11,3},{4,12},{12,4},... | collective-permute-start | bytes 6291464 | tf_op jit(solution)/shard_map/ppermute | solution.py:249
  72.7 4.2 %collective-permute-done = bf16[4096,256]{1,0:T(8,128)(2,1)S(1)} collective-permute-done((bf16[4096,256]{1,0:T(8,128)(2,1)}, bf16[4096,256]{1,0:T(8,128)(2,1)S(1)}, u32[]{:S(2)}, u32[]{:S(2)}) %collective-permute-start) | collective-permute-done | bytes 2097184 | tf_op jit(solution)/shard_map/ppermute | solution.py:249
  77.0 1.6 copy-done
  78.5 1.6 copy-done.5
  80.1 3.3 %attention.2 = (bf16[256,256]{1,0:T(8,128)(2,1)S(1)}, bf16[2,2,256,256]{3,2,1,0:T(8,128)(2,1)}) custom-call(s32[3]{0:T(128)S(1)} %pad_add_fusion.info, s32[2]{0:T(128)S(1)} %get-tuple-element.25.starts, s32[2]{0:T(128)S(1)} %get-tuple-element.24.stops, bf16[8,256,256]{2,1,0:T(8,128)(2,1)S(1)} %all_to_all.31.x_ref.gs_ref, ...), custom_call_target="tpu_custom_call" | custom-call | flops 1107296256 | bytes 6291456 | tf_op jit(solution)/shard_map/attention/pallas_call | solution.py:137
  83.5 1.3 copy-done.2
  84.8 1.1 broadcast_in_dim.28
  85.8 5.7 %all-to-all-start.2 = ((bf16[8,256,256]{2,1,0:T(8,128)(2,1)}), bf16[8,256,256]{2,1,0:T(8,128)(2,1)S(1)}, u32[]{:S(2)}, u32[]{:S(2)}) async-start(bf16[8,256,256]{2,1,0:T(8,128)(2,1)} %broadcast_in_dim.28), calls=%async_computation.2 | async-start | bytes 2097152 | tf_op jit(solution)/shard_map/all_to_all | solution.py:27
  91.7 0.1 maximum_maximum_fusion.gs_ref
  91.8 14.6 %all-to-all-done.2.att = bf16[8,256,256]{2,1,0:T(8,128)(2,1)S(1)} async-done(((bf16[8,256,256]{2,1,0:T(8,128)(2,1)}), bf16[8,256,256]{2,1,0:T(8,128)(2,1)S(1)}, u32[]{:S(2)}, u32[]{:S(2)}) %all-to-all-start.2) | async-done | bytes 1048608 | tf_op jit(solution)/shard_map/all_to_all | solution.py:27
  106.4 1.6 copy-done.3
  108.0 1.0 project.2
  109.1 19.3 %all_to_all.32.x_ref.gs_ref = bf16[8,272,256]{2,1,0:T(8,128)(2,1)S(1)} all-to-all(bf16[8,272,256]{2,1,0:T(8,128)(2,1)S(1)} %broadcast_in_dim.66), channel_id=1, replica_groups=mesh['z'=8,'yh'=4,'c'=2,'x'=4,'yl'=2] {'x','yl'}, dimensions={0} | all-to-all | bytes 2228224 | tf_op jit(solution)/shard_map/all_to_all | solution.py:27
  128.4 4.3 %attention.3 = (bf16[256,256]{1,0:T(8,128)(2,1)S(1)}, bf16[2,2,256,256]{3,2,1,0:T(8,128)(2,1)}, bf16[256,256]{1,0:T(8,128)(2,1)S(1)}) custom-call(s32[3]{0:T(128)S(1)} %pad_add_fusion.info, s32[2]{0:T(128)S(1)} %get-tuple-element.25.starts, s32[2]{0:T(128)S(1)} %get-tuple-element.24.stops, ...), custom_call_target="tpu_custom_call", output_to_operand_aliasing={{1}: (7, {})} | custom-call | flops 1107296256 | bytes 6291456 | tf_op jit(solution)/shard_map/attention/pallas_call | solution.py:137
  132.8 17.5 %all_to_all.33.att = bf16[8,256,256]{2,1,0:T(8,128)(2,1)S(1)} all-to-all(bf16[8,256,256]{2,1,0:T(8,128)(2,1)S(1)} %broadcast_in_dim.67), channel_id=1, replica_groups=mesh['z'=8,'yh'=4,'c'=2,'x'=4,'yl'=2] {'x','yl'}, dimensions={0} | all-to-all | bytes 2097152 | tf_op jit(solution)/shard_map/all_to_all | solution.py:27
  150.3 1.2 project.3
  151.5 0.7 copy-done.8
  152.2 9.3 %all_to_all.34.stats = f32[8,8,256]{2,1,0:T(8,128)} all-to-all(f32[8,8,256]{2,1,0:T(8,128)S(1)} %broadcast_in_dim.68), channel_id=1, replica_groups=mesh['z'=8,'yh'=4,'c'=2,'x'=4,'yl'=2] {'x','yl'}, dimensions={0} | all-to-all | bytes 131072 | tf_op jit(solution)/shard_map/all_to_all | solution.py:27
  161.4 1.8 %finish.1 = bf16[256,256]{1,0:T(8,128)(2,1)} custom-call(f32[8,8,256]{2,1,0:T(8,128)} %all_to_all.34.stats, bf16[256,256]{1,0:T(8,128)(2,1)} %copy-done.8, bf16[1,256]{1,0:T(2,128)(2,1)} %copy-done.9, bf16[1,256]{1,0:T(2,128)(2,1)} %copy-done.10), custom_call_target="tpu_custom_call" | custom-call | tf_op jit(solution)/shard_map/finish/pallas_call | solution.py:214
  (44 shorter events, 0.5 us)
Async XLA Ops:
  7.2 63.5 %all-gather.2.cloned.1.call-start = ((), (), s32[]{:S(2)}) async-start(), calls=%async_computation.6 | async-start | bytes 2359296 | tf_op jit(solution)/shard_map/all_gather | solution.py:246
  8.1 64.6 %copy-start.11 = (bf16[3,256]{1,0:T(4,128)(2,1)S(1)}, bf16[3,256]{1,0:T(4,128)(2,1)}, u32[]{:S(2)}) copy-start(bf16[3,256]{1,0:T(4,128)(2,1)} %param.15) | copy-start | bytes 4612
  8.1 64.6 %copy-start.12 = (s32[2]{0:T(128)S(1)}, s32[2]{0:T(128)}, u32[]{:S(2)}) copy-start(s32[2]{0:T(128)} %param.11) | copy-start | bytes 28
  8.1 64.6 %copy-start.13 = (s32[2]{0:T(128)S(1)}, s32[2]{0:T(128)}, u32[]{:S(2)}) copy-start(s32[2]{0:T(128)} %param.12) | copy-start | bytes 28
  70.7 6.3 %collective-permute-start = (bf16[4096,256]{1,0:T(8,128)(2,1)}, bf16[4096,256]{1,0:T(8,128)(2,1)S(1)}, u32[]{:S(2)}, u32[]{:S(2)}) collective-permute-start(bf16[4096,256]{1,0:T(8,128)(2,1)} %all-gather.2.cloned.1.call-done), channel_id=1, source_target_pairs={{0,8},{8,0},{1,9},{9,1},{2,10},{10,2},{3,11},{11,3},{4,12},{12,4},... | collective-permute-start | bytes 6291464 | tf_op jit(solution)/shard_map/ppermute | solution.py:249
  77.0 1.6 copy-start
  78.5 1.6 copy-start.5
  83.4 1.3 copy-start.2
  84.7 6.8 %copy-start.15 = (bf16[256]{0:T(256)(128)(2,1)S(1)}, bf16[256]{0:T(256)(128)(2,1)}, u32[]{:S(2)}) copy-start(bf16[256]{0:T(256)(128)(2,1)} %param.18) | copy-start | bytes 1540
  84.8 6.8 %copy-start.16 = (bf16[256]{0:T(256)(128)(2,1)S(1)}, bf16[256]{0:T(256)(128)(2,1)}, u32[]{:S(2)}) copy-start(bf16[256]{0:T(256)(128)(2,1)} %param.19) | copy-start | bytes 1540
  84.8 21.6 %copy-start.14 = (bf16[256]{0:T(256)(128)(2,1)S(1)}, bf16[256]{0:T(256)(128)(2,1)}, u32[]{:S(2)}) copy-start(bf16[256]{0:T(256)(128)(2,1)} %param.17) | copy-start | bytes 1540
  84.8 21.7 %copy-start.1 = (bf16[4096,256]{1,0:T(8,128)(2,1)S(1)}, bf16[4096,256]{1,0:T(8,128)(2,1)}, u32[]{:S(2)}) copy-start(bf16[4096,256]{1,0:T(8,128)(2,1)} %all-gather.2.cloned.1.call-done) | copy-start | bytes 6291460
  84.8 21.7 %copy-start.7 = (bf16[256,256]{1,0:T(8,128)(2,1)S(1)}, bf16[256,256]{1,0:T(8,128)(2,1)}, u32[]{:S(2)}) copy-start(bf16[256,256]{1,0:T(8,128)(2,1)} %res_ref.1) | copy-start | bytes 393220
  85.8 20.6 %all-to-all-start.2 = ((bf16[8,256,256]{2,1,0:T(8,128)(2,1)}), bf16[8,256,256]{2,1,0:T(8,128)(2,1)S(1)}, u32[]{:S(2)}, u32[]{:S(2)}) async-start(bf16[8,256,256]{2,1,0:T(8,128)(2,1)} %broadcast_in_dim.28), calls=%async_computation.2 | async-start | bytes 2097152 | tf_op jit(solution)/shard_map/all_to_all | solution.py:27
  91.6 17.4 %copy-start.9 = (bf16[1,256]{1,0:T(2,128)(2,1)}, bf16[1,256]{1,0:T(2,128)(2,1)S(1)}, u32[]{:S(2)}) copy-start(bf16[1,256]{1,0:T(2,128)(2,1)S(1)} %broadcast_in_dim.30.gain_ref) | copy-start | bytes 1540
  91.6 17.4 %copy-start.10 = (bf16[1,256]{1,0:T(2,128)(2,1)}, bf16[1,256]{1,0:T(2,128)(2,1)S(1)}, u32[]{:S(2)}) copy-start(bf16[1,256]{1,0:T(2,128)(2,1)S(1)} %broadcast_in_dim.31.shift_ref) | copy-start | bytes 1540
  106.4 1.6 copy-start.3
  108.0 20.4 %copy-start.6 = (bf16[2,2,1024,256]{3,2,1,0:T(8,128)(2,1)S(1)}, bf16[2,2,1024,256]{3,2,1,0:T(8,128)(2,1)}, u32[]{:S(2)}) copy-start(bf16[2,2,1024,256]{3,2,1,0:T(8,128)(2,1)} %cache.3) | copy-start | bytes 6291460
  109.0 19.4 %copy-start.4 = (bf16[4096,256]{1,0:T(8,128)(2,1)S(1)}, bf16[4096,256]{1,0:T(8,128)(2,1)}, u32[]{:S(2)}) copy-start(bf16[4096,256]{1,0:T(8,128)(2,1)} %copy-done.2) | copy-start | bytes 6291460
  151.5 0.7 copy-start.8
Sparse Core Ops, SparseCore 0:
  20.9 49.7 all-gather.1

commit v2 on v1

v2 whole, which is shorter than its diff:
```python
import functools
import math

import jax
import jax.numpy as jnp
from jax import lax
from jax.experimental import pallas as pl
from jax.experimental.pallas import tpu as pltpu
from jax.sharding import Mesh
from jax.sharding import PartitionSpec as P

HEAD = 128
SPAN = 128
EPSILON = 1e-05
NEGATIVE = -1e30
AXES = ("zh", "zl", "yh", "c", "x", "yl")
SIZES = (4, 2, 4, 2, 4, 2)
WIDE = ("zh", "zl", "yh", "c")
NARROW = ("x", "yl")
SWAP = [(0, 1), (1, 0)]
VMEM_LIMIT = 16 * 1024 * 1024
F32 = jnp.float32
BF16 = jnp.bfloat16


def spread(x, axes, count):
    return lax.all_to_all(jnp.broadcast_to(x[None], (count,) + x.shape), axes, 0, 0, tiled=True)


def dot(a, b):
    return jnp.dot(a, b, preferred_element_type=F32)


def dot_t(a, b):
    return lax.dot_general(a, b, (((1,), (1,)), ((), ())), preferred_element_type=F32)


def rows_of(pieces, info, z, j):
    same, same_swap, away, away_swap = pieces
    zh, zl = z // 2, z % 2
    low = info[0] == 0
    here = info[1] == zl
    parts = []
    for y in range(4):
        mine = jnp.where(here, same[zh, y, j], away[zh, y, j])
        theirs = jnp.where(here, same_swap[zh, y, j], away_swap[zh, y, j])
        parts += [jnp.where(low, mine, theirs), jnp.where(low, theirs, mine)]
    return jnp.concatenate(parts, axis=0)


def attention_kernel(layer, info, starts, stops, params, cache_ref, prev, *rest):
    pieces, rest = rest[:4], rest[4:]
    count = 4 if layer == 0 else 2
    inputs, rest = rest[:count], rest[count:]
    att_ref, new_ref, extra_ref, new, cache, sems, x = rest
    fetch = pltpu.make_async_copy(cache_ref.at[layer], cache, sems.at[2])
    fetch.start()
    if layer == 0:
        for k in range(8):
            source = info[2] ^ k
            x[source] = inputs[k // 2][k % 2, 0:256, :]
            extra_ref[source] = inputs[k // 2][k % 2, 256:272, :]
    else:
        x_ref, gs_ref = inputs
        total = jnp.zeros((256, 1), F32)
        for n in range(8):
            total += jnp.sum(x_ref[n].astype(F32), axis=1, keepdims=True)
        mean = total / 2048.0
        spread_sum = jnp.zeros((256, 1), F32)
        for n in range(8):
            centered = x_ref[n].astype(F32) - mean
            spread_sum += jnp.sum(centered * centered, axis=1, keepdims=True)
        scale = lax.rsqrt(spread_sum / 2048.0 + EPSILON)
        for n in range(8):
            both = gs_ref[n].astype(F32)
            normed = (x_ref[n].astype(F32) - mean) * scale * both[0:1] + both[1:2]
            x[n] = normed.astype(BF16)
        extra_ref[...] = x[info[2]]
    bias = params[...]
    parts = []
    copies = []
    for j in range(3):
        acc = dot(x[0], rows_of(pieces, info, 0, j))
        for n in range(1, 8):
            acc += dot(x[n], rows_of(pieces, info, n, j))
        parts.append((acc + bias[j : j + 1]).astype(BF16))
        if j > 0:
            new[j - 1] = parts[j]
            copy = pltpu.make_async_copy(new.at[j - 1], new_ref.at[layer, j - 1], sems.at[j - 1])
            copy.start()
            copies.append(copy)
    q, k_new, v_new = parts
    fetch.wait()
    factor = 1.0 / math.sqrt(HEAD)
    column = lax.broadcasted_iota(jnp.int32, (1, 1024), 1)
    causal = lax.broadcasted_iota(jnp.int32, (SPAN, SPAN), 0) >= lax.broadcasted_iota(
        jnp.int32, (SPAN, SPAN), 1
    )
    for r in range(2):
        rows = slice(r * SPAN, (r + 1) * SPAN)
        live = (column >= starts[r]) & (column < stops[r])
        for h in range(2):
            cols = slice(h * HEAD, (h + 1) * HEAD)
            qh = q[rows, cols]
            sc = jnp.where(live, dot_t(qh, cache[0, :, cols]) * factor, NEGATIVE)
            sn = jnp.where(causal, dot_t(qh, k_new[rows, cols]) * factor, NEGATIVE)
            top = jnp.maximum(
                jnp.max(sc, axis=1, keepdims=True), jnp.max(sn, axis=1, keepdims=True)
            )
            pc = jnp.exp(sc - top)
            pn = jnp.exp(sn - top)
            norm = jnp.sum(pc, axis=1, keepdims=True) + jnp.sum(pn, axis=1, keepdims=True)
            out = dot(pc.astype(BF16), cache[1, :, cols]) + dot(
                pn.astype(BF16), v_new[rows, cols]
            )
            att_ref[rows, cols] = (out / norm).astype(BF16)
    for copy in copies:
        copy.wait()


def attention(layer, info, starts, stops, params, cache, prev, pieces, inputs):
    smem = pl.BlockSpec(memory_space=pltpu.SMEM)
    vmem = pl.BlockSpec(memory_space=pltpu.VMEM)
    anywhere = pl.BlockSpec(memory_space=pl.ANY)
    tile = jax.ShapeDtypeStruct((256, 256), BF16)
    vectors = jax.ShapeDtypeStruct((8, 16, 256), BF16)
    out_shape = [
        tile,
        jax.ShapeDtypeStruct((2, 2, 256, 256), BF16),
        vectors if layer == 0 else tile,
    ]
    return pl.pallas_call(
        functools.partial(attention_kernel, layer),
        out_shape=out_shape,
        in_specs=[smem] * 3 + [vmem, anywhere, anywhere] + [vmem] * (4 + len(inputs)),
        out_specs=[vmem, anywhere, vmem],
        scratch_shapes=[
            pltpu.VMEM((2, 256, 256), BF16),
            pltpu.VMEM((2, 1024, 256), BF16),
            pltpu.SemaphoreType.DMA((3,)),
            pltpu.VMEM((8, 256, 256), BF16),
        ],
        input_output_aliases={5: 1} if layer > 0 else {},
        compiler_params=pltpu.CompilerParams(vmem_limit_bytes=VMEM_LIMIT),
        cost_estimate=pl.CostEstimate(
            flops=2 * 256 * 2048 * 768 + 4 * 256 * 1152 * 256,
            bytes_accessed=6 << 20,
            transcendentals=256 * 1152 * 2,
        ),
        name="attention",
    )(info, starts, stops, params, cache, prev, *pieces, *inputs)


def project_kernel(last, info, att, params, res_ref, *rest):
    pieces, out_ref = rest[:4], rest[4]
    acc = dot(att[0], rows_of(pieces, info, 0, 3))
    for n in range(1, 8):
        acc += dot(att[n], rows_of(pieces, info, n, 3))
    bias = params[...]
    summed = (acc + bias[3:4] + res_ref[...].astype(F32)).astype(BF16)
    out_ref[...] = summed
    if last:
        values = summed.astype(F32)
        mean = jnp.sum(values, axis=1, keepdims=True) / 256.0
        centered = values - mean
        spread_sum = jnp.sum(centered * centered, axis=1, keepdims=True)
        lane = lax.broadcasted_iota(jnp.int32, (256, 128), 1)
        stats = jnp.where(lane == 0, mean, spread_sum)
        rest[5][...] = stats.T[0:8, :]


def project(last, info, att, params, res, pieces):
    vmem = pl.BlockSpec(memory_space=pltpu.VMEM)
    out_shape = [jax.ShapeDtypeStruct((256, 256), BF16)]
    if last:
        out_shape.append(jax.ShapeDtypeStruct((8, 256), F32))
    return pl.pallas_call(
        functools.partial(project_kernel, last),
        out_shape=out_shape,
        in_specs=[pl.BlockSpec(memory_space=pltpu.SMEM)] + [vmem] * 7,
        out_specs=[vmem] * len(out_shape),
        compiler_params=pltpu.CompilerParams(vmem_limit_bytes=VMEM_LIMIT),
        cost_estimate=pl.CostEstimate(
            flops=2 * 256 * 2048 * 256, bytes_accessed=3 << 20, transcendentals=0
        ),
        name="project",
    )(info, att, params, res, *pieces)


def finish_kernel(stats, summed, params, out_ref):
    means = [stats[n, 0:1, :] for n in range(8)]
    mean = functools.reduce(lambda a, b: a + b, means) / 8.0
    total = jnp.zeros((1, 256), F32)
    for n in range(8):
        offset = means[n] - mean
        total += stats[n, 1:2, :] + 256.0 * offset * offset
    scale = lax.rsqrt(total / 2048.0 + EPSILON)
    row = lax.broadcasted_iota(jnp.int32, (128, 256), 0)
    columns = jnp.where(row == 0, mean, scale).T
    values = summed[...].astype(F32)
    scaled = (values - columns[:, 0:1]) * columns[:, 1:2]
    gains = params[...]
    out_ref[...] = (scaled * gains[4:5] + gains[5:6]).astype(BF16)


def finish(stats, summed, params):
    vmem = pl.BlockSpec(memory_space=pltpu.VMEM)
    return pl.pallas_call(
        finish_kernel,
        out_shape=jax.ShapeDtypeStruct((256, 256), BF16),
        in_specs=[vmem] * 3,
        out_specs=vmem,
        compiler_params=pltpu.CompilerParams(vmem_limit_bytes=VMEM_LIMIT),
        name="finish",
    )(stats, summed, params)


def shards(
    hidden_in,
    cache_lengths,
    cache_offsets,
    cache_kv,
    w_qkv,
    qkv_bias,
    w_out,
    out_bias,
    norm_gain,
    norm_shift,
):
    cache_count = cache_kv.shape[2]
    info = jnp.stack([lax.axis_index("c"), lax.axis_index("zl"), lax.axis_index(NARROW)])
    starts = cache_offsets - lax.axis_index(WIDE) * cache_count
    stops = starts + cache_lengths
    vectors = [qkv_bias, out_bias[None], norm_gain[None], norm_shift[None]]
    params = jnp.pad(jnp.concatenate(vectors, axis=0).astype(F32), ((0, 2), (0, 0)))
    payload = jnp.concatenate(
        [hidden_in, norm_gain[None], norm_shift[None], jnp.zeros((14, 256), BF16)], axis=0
    )

    pieces = jnp.concatenate([w_qkv.transpose(1, 0, 2), w_out[None]], axis=0)
    near = spread(pieces, "yh", 4)
    near, payload = lax.optimization_barrier((near, payload))
    same = spread(near, "zh", 4)
    blocks = jnp.stack([payload, lax.ppermute(payload, "yl", SWAP)])
    blocks = [blocks] + [
        lax.ppermute(blocks, "x", [(i, i ^ k) for i in range(4)]) for k in range(1, 4)
    ]
    same, blocks, params, info, starts, stops = lax.optimization_barrier(
        (same, blocks, params, info, starts, stops)
    )
    left = lax.ppermute(same[:2], ("zh", "zl"), [(i, (i + 1) % 8) for i in range(8)])
    right = lax.ppermute(same[2:], ("zh", "zl"), [(i, (i - 1) % 8) for i in range(8)])
    same_swap = lax.ppermute(same, "c", SWAP)
    away = jnp.concatenate([left, right], axis=0)
    pieces = [same, same_swap, away, lax.ppermute(away, "c", SWAP)]

    blank = jnp.zeros((8, 128), BF16)
    att, new_cache, vectors = attention(
        0, info, starts, stops, params, cache_kv, blank, pieces, blocks
    )
    heads = spread(att, NARROW, 8)
    (summed,) = project(False, info, heads, params, hidden_in, pieces)
    rows = spread(summed, NARROW, 8)
    att, new_cache, carried = attention(
        1, info, starts, stops, params, cache_kv, new_cache, pieces, [rows, vectors]
    )
    heads = spread(att, NARROW, 8)
    summed, stats = project(True, info, heads, params, carried, pieces)
    hidden_out = finish(spread(stats, NARROW, 8), summed, params)
    return hidden_out, new_cache


def solution(mesh):
    split = Mesh(mesh.devices.reshape(SIZES), AXES)
    in_specs = (
        P(WIDE, NARROW),
        P(WIDE),
        P(WIDE),
        P(None, None, WIDE, NARROW),
        P(WIDE, None, NARROW),
        P(None, NARROW),
        P(WIDE, NARROW),
        P(NARROW),
        P(NARROW),
        P(NARROW),
    )
    out_specs = (P(WIDE, NARROW), P(None, None, WIDE, NARROW))
    return jax.shard_map(shards, mesh=split, in_specs=in_specs, out_specs=out_specs, check_vma=False)
```

time: 172 us -> 158 us (0.919)
  the two profiles are of different devices: /device:TPU:56 before, /device:TPU:16 now
where the time goes in v2:
time: 158 us; the launch traced here: 157 us
  blocking collectives  63.7 us (40%)
  starting transfers between devices  43.7 us (28%)
  waiting for transfers between devices  31.3 us (20%)
  Pallas kernels  12 us (8%)
  local copies, waits for them, and re-layouts  3.66 us (2%)
  other arithmetic  1.98 us (1%)
    all_to_all x4, blocking collectives, spread(): lax.all_to_all(jnp.broadcast_to(x[None], (count,) + x.shape), axes, 0, 0,...  63.7 us
    all_to_all x2, starting transfers between devices, spread(): lax.all_to_all(jnp.broadcast_to(x[None], (count,) + x.shape), axes, 0, 0,...  19.5 us
    ppermute x3, starting transfers between devices, shards(): lax.ppermute(blocks, 'x', [(i, i ^ k) for i in range(4)])  9.82 us
    pallas_call x2, Pallas kernels, attention(): pl.pallas_call(functools.partial(attention_kernel, layer), out_shape=out_...  8.8 us
    ppermute x3, waiting for transfers between devices, shards(): lax.ppermute(blocks, 'x', [(i, i ^ k) for i in range(4)])  8.57 us
    ppermute x1, waiting for transfers between devices, shards(): lax.ppermute(same[:2], ('zh', 'zl'), [(i, (i + 1) % 8) for i in range(8)])  6.93 us
    ppermute x1, starting transfers between devices, shards(): lax.ppermute(same[:2], ('zh', 'zl'), [(i, (i + 1) % 8) for i in range(8)])  5.79 us
    all_to_all x2, waiting for transfers between devices, spread(): lax.all_to_all(jnp.broadcast_to(x[None], (count,) + x.shape), axes, 0, 0,...  5.43 us
  transfers between devices with their start and end apart: 10, of which 8 were waited for; matrix products, arithmetic and copies ran while one was open for 2% of the time, Pallas kernels for 0%

profile of v2, /device:TPU:16, one launch (start us, length us, event | category | flops | bytes accessed | tf_op | source)
XLA Modules:
  0.0 157.2 jit_solution(73449917904785309)
XLA Ops:
  2.2 9.2 %all-to-all-start = ((bf16[4,4,32,256]{3,2,1,0:T(8,128)(2,1)}), bf16[4,4,32,256]{3,2,1,0:T(8,128)(2,1)S(1)}, u32[]{:S(2)}, u32[]{:S(2)}) async-start(bf16[4,4,32,256]{3,2,1,0:T(8,128)(2,1)} %broadcast_in_dim.25), calls=%async_computation | async-start | bytes 524288 | tf_op jit(solution)/shard_map/all_to_all | solution.py:27
  13.8 5.4 %all-to-all-done = bf16[4,4,32,256]{3,2,1,0:T(8,128)(2,1)S(1)} async-done(((bf16[4,4,32,256]{3,2,1,0:T(8,128)(2,1)}), bf16[4,4,32,256]{3,2,1,0:T(8,128)(2,1)S(1)}, u32[]{:S(2)}, u32[]{:S(2)}) %all-to-all-start) | async-done | bytes 262176 | tf_op jit(solution)/shard_map/all_to_all | solution.py:27
  20.4 10.3 %all-to-all-start.1 = ((bf16[4,4,4,32,256]{4,3,2,1,0:T(8,128)(2,1)}), bf16[4,4,4,32,256]{4,3,2,1,0:T(8,128)(2,1)S(1)}, u32[]{:S(2)}, u32[]{:S(2)}) async-start(bf16[4,4,4,32,256]{4,3,2,1,0:T(8,128)(2,1)} %broadcast_in_dim.29), calls=%async_computation.1 | async-start | bytes 2097152 | tf_op jit(solution)/shard_map/all_to_all | solution.py:27
  30.7 2.4 %collective-permute-start = (bf16[272,256]{1,0:T(8,128)(2,1)S(1)}, bf16[272,256]{1,0:T(8,128)(2,1)S(1)}, u32[]{:S(2)}, u32[]{:S(2)}) collective-permute-start(bf16[272,256]{1,0:T(8,128)(2,1)S(1)} %maximum_maximum_fusion), channel_id=1, source_target_pairs={{0,1},{1,0},{2,3},{3,2},{4,5},{5,4},{6,7},{7,6},{8,9},{9,8},{10,11... | collective-permute-start | bytes 417800 | tf_op jit(solution)/shard_map/ppermute | solution.py:244
  33.2 4.5 %collective-permute-done = bf16[272,256]{1,0:T(8,128)(2,1)S(1)} collective-permute-done((bf16[272,256]{1,0:T(8,128)(2,1)S(1)}, bf16[272,256]{1,0:T(8,128)(2,1)S(1)}, u32[]{:S(2)}, u32[]{:S(2)}) %collective-permute-start) | collective-permute-done | bytes 139296 | tf_op jit(solution)/shard_map/ppermute | solution.py:244
  37.7 4.7 %collective-permute-start.3 = (bf16[2,272,256]{2,1,0:T(8,128)(2,1)S(1)}, bf16[2,272,256]{2,1,0:T(8,128)(2,1)S(1)}, u32[]{:S(2)}, u32[]{:S(2)}) collective-permute-start(bf16[2,272,256]{2,1,0:T(8,128)(2,1)S(1)} %pad_maximum_fusion.rest_4_), channel_id=1, source_target_pairs={{0,6},{2,4},{4,2},{6,0},{1,7},{3,5},{5,3},{7,1},{8,14},{10,12},{12... | collective-permute-start | bytes 835592 | tf_op jit(solution)/shard_map/ppermute | solution.py:246
  42.4 2.7 %collective-permute-start.2 = (bf16[2,272,256]{2,1,0:T(8,128)(2,1)S(1)}, bf16[2,272,256]{2,1,0:T(8,128)(2,1)S(1)}, u32[]{:S(2)}, u32[]{:S(2)}) collective-permute-start(bf16[2,272,256]{2,1,0:T(8,128)(2,1)S(1)} %pad_maximum_fusion.rest_4_), channel_id=1, source_target_pairs={{0,4},{2,6},{4,0},{6,2},{1,5},{3,7},{5,1},{7,3},{8,12},{10,14},{12... | collective-permute-start | bytes 835592 | tf_op jit(solution)/shard_map/ppermute | solution.py:246
  45.1 2.4 %collective-permute-start.1 = (bf16[2,272,256]{2,1,0:T(8,128)(2,1)S(1)}, bf16[2,272,256]{2,1,0:T(8,128)(2,1)S(1)}, u32[]{:S(2)}, u32[]{:S(2)}) collective-permute-start(bf16[2,272,256]{2,1,0:T(8,128)(2,1)S(1)} %pad_maximum_fusion.rest_4_), channel_id=1, source_target_pairs={{0,2},{2,0},{4,6},{6,4},{1,3},{3,1},{5,7},{7,5},{8,10},{10,8},{12,... | collective-permute-start | bytes 835592 | tf_op jit(solution)/shard_map/ppermute | solution.py:246
  47.6 5.1 %collective-permute-done.3.rest_7_ = bf16[2,272,256]{2,1,0:T(8,128)(2,1)S(1)} collective-permute-done((bf16[2,272,256]{2,1,0:T(8,128)(2,1)S(1)}, bf16[2,272,256]{2,1,0:T(8,128)(2,1)S(1)}, u32[]{:S(2)}, u32[]{:S(2)}) %collective-permute-start.3) | collective-permute-done | bytes 278560 | tf_op jit(solution)/shard_map/ppermute | solution.py:246
  52.7 2.6 %collective-permute-done.2.rest_6_ = bf16[2,272,256]{2,1,0:T(8,128)(2,1)S(1)} collective-permute-done((bf16[2,272,256]{2,1,0:T(8,128)(2,1)S(1)}, bf16[2,272,256]{2,1,0:T(8,128)(2,1)S(1)}, u32[]{:S(2)}, u32[]{:S(2)}) %collective-permute-start.2) | collective-permute-done | bytes 278560 | tf_op jit(solution)/shard_map/ppermute | solution.py:246
  56.3 5.8 %collective-permute-start.5 = (bf16[2,4,4,32,256]{4,3,2,1,0:T(8,128)(2,1)S(1)}, bf16[2,4,4,32,256]{4,3,2,1,0:T(8,128)(2,1)S(1)}, u32[]{:S(2)}, u32[]{:S(2)}) collective-permute-start(bf16[2,4,4,32,256]{4,3,2,1,0:T(8,128)(2,1)S(1)} %get-tuple-element.43), channel_id=1, source_target_pairs={{0,64},{64,128},{128,192},{192,256},{256,320},{320,384},{384,448},... | collective-permute-start | bytes 1572872 | tf_op jit(solution)/shard_map/ppermute | solution.py:251
  62.1 2.3 %collective-permute-start.6 = (bf16[2,4,4,32,256]{4,3,2,1,0:T(8,128)(2,1)S(1)}, bf16[2,4,4,32,256]{4,3,2,1,0:T(8,128)(2,1)S(1)}, u32[]{:S(2)}, u32[]{:S(2)}) collective-permute-start(bf16[2,4,4,32,256]{4,3,2,1,0:T(8,128)(2,1)S(1)} %get-tuple-element.42), channel_id=1, source_target_pairs={{0,448},{64,0},{128,64},{192,128},{256,192},{320,256},{384,320},{4... | collective-permute-start | bytes 1572872 | tf_op jit(solution)/shard_map/ppermute | solution.py:252
  64.4 1.9 %collective-permute-start.4 = (bf16[4,4,4,32,256]{4,3,2,1,0:T(8,128)(2,1)S(1)}, bf16[4,4,4,32,256]{4,3,2,1,0:T(8,128)(2,1)S(1)}, u32[]{:S(2)}, u32[]{:S(2)}) collective-permute-start(bf16[4,4,4,32,256]{4,3,2,1,0:T(8,128)(2,1)S(1)} %all-to-all-done.1.rest_0_), channel_id=1, source_target_pairs={{0,8},{8,0},{1,9},{9,1},{2,10},{10,2},{3,11},{11,3},{4,12},{12,4},... | collective-permute-start | bytes 3145736 | tf_op jit(solution)/shard_map/ppermute | solution.py:253
  66.3 6.9 %collective-permute-done.5 = bf16[2,4,4,32,256]{4,3,2,1,0:T(8,128)(2,1)S(1)} collective-permute-done((bf16[2,4,4,32,256]{4,3,2,1,0:T(8,128)(2,1)S(1)}, bf16[2,4,4,32,256]{4,3,2,1,0:T(8,128)(2,1)S(1)}, u32[]{:S(2)}, u32[]{:S(2)}) %collective-permute-start.5) | collective-permute-done | bytes 524320 | tf_op jit(solution)/shard_map/ppermute | solution.py:251
  73.3 3.3 %collective-permute-done.6 = bf16[2,4,4,32,256]{4,3,2,1,0:T(8,128)(2,1)S(1)} collective-permute-done((bf16[2,4,4,32,256]{4,3,2,1,0:T(8,128)(2,1)S(1)}, bf16[2,4,4,32,256]{4,3,2,1,0:T(8,128)(2,1)S(1)}, u32[]{:S(2)}, u32[]{:S(2)}) %collective-permute-start.6) | collective-permute-done | bytes 524320 | tf_op jit(solution)/shard_map/ppermute | solution.py:252
  76.7 1.9 %collective-permute-start.7 = (bf16[4,4,4,32,256]{4,3,2,1,0:T(8,128)(2,1)S(1)}, bf16[4,4,4,32,256]{4,3,2,1,0:T(8,128)(2,1)S(1)}, u32[]{:S(2)}, u32[]{:S(2)}) collective-permute-start(bf16[4,4,4,32,256]{4,3,2,1,0:T(8,128)(2,1)S(1)} %constant_dynamic-update-slice_fusion.rest_2_), channel_id=1, source_target_pairs={{0,8},{8,0},{1,9},{9,1},{2,10},{10,2},{3,11},{11,3},{4,12},{12,4},... | collective-permute-start | bytes 3145736 | tf_op jit(solution)/shard_map/ppermute | solution.py:255
  78.6 2.6 %collective-permute-done.7.rest_3_ = bf16[4,4,4,32,256]{4,3,2,1,0:T(8,128)(2,1)S(1)} collective-permute-done((bf16[4,4,4,32,256]{4,3,2,1,0:T(8,128)(2,1)S(1)}, bf16[4,4,4,32,256]{4,3,2,1,0:T(8,128)(2,1)S(1)}, u32[]{:S(2)}, u32[]{:S(2)}) %collective-permute-start.7) | collective-permute-done | bytes 1048608 | tf_op jit(solution)/shard_map/ppermute | solution.py:255
  81.2 3.9 %attention.2 = (bf16[256,256]{1,0:T(8,128)(2,1)S(1)}, bf16[2,2,256,256]{3,2,1,0:T(8,128)(2,1)}, bf16[8,16,256]{2,1,0:T(8,128)(2,1)S(1)}) custom-call(s32[3]{0:T(128)S(1)} %pad_add_fusion.info, s32[2]{0:T(128)S(1)} %get-tuple-element.24.starts, s32[2]{0:T(128)S(1)} %get-tuple-element.25.stops, f32[8,256]{1,0:T(8,128)S(1)} %fusion.7.params, ...), custom_call_target="tpu_custom_call" | custom-call | flops 1107296256 | bytes 6291456 | tf_op jit(solution)/shard_map/attention/pallas_call | solution.py:132
  85.2 20.1 %all_to_all.30.att = bf16[8,256,256]{2,1,0:T(8,128)(2,1)S(1)} all-to-all(bf16[8,256,256]{2,1,0:T(8,128)(2,1)S(1)} %broadcast_in_dim.64), channel_id=1, replica_groups=mesh['zh'=4,'zl'=2,'yh'=4,'c'=2,'x'=4,'yl'=2] {'x','yl'}, dimensions={0} | all-to-all | bytes 2097152 | tf_op jit(solution)/shard_map/all_to_all | solution.py:27
  106.5 17.7 %all_to_all.31.rest_4_ = bf16[8,256,256]{2,1,0:T(8,128)(2,1)S(1)} all-to-all(bf16[8,256,256]{2,1,0:T(8,128)(2,1)S(1)} %broadcast_in_dim.65), channel_id=1, replica_groups=mesh['zh'=4,'zl'=2,'yh'=4,'c'=2,'x'=4,'yl'=2] {'x','yl'}, dimensions={0} | all-to-all | bytes 2097152 | tf_op jit(solution)/shard_map/all_to_all | solution.py:27
  124.2 4.9 %attention.3 = (bf16[256,256]{1,0:T(8,128)(2,1)S(1)}, bf16[2,2,256,256]{3,2,1,0:T(8,128)(2,1)}, bf16[256,256]{1,0:T(8,128)(2,1)S(1)}) custom-call(s32[3]{0:T(128)S(1)} %pad_add_fusion.info, s32[2]{0:T(128)S(1)} %get-tuple-element.24.starts, s32[2]{0:T(128)S(1)} %get-tuple-element.25.stops, ...), custom_call_target="tpu_custom_call", output_to_operand_aliasing={{1}: (5, {})} | custom-call | flops 1107296256 | bytes 6291456 | tf_op jit(solution)/shard_map/attention/pallas_call | solution.py:132
  129.1 17.0 %all_to_all.32.att = bf16[8,256,256]{2,1,0:T(8,128)(2,1)S(1)} all-to-all(bf16[8,256,256]{2,1,0:T(8,128)(2,1)S(1)} %broadcast_in_dim.66), channel_id=1, replica_groups=mesh['zh'=4,'zl'=2,'yh'=4,'c'=2,'x'=4,'yl'=2] {'x','yl'}, dimensions={0} | all-to-all | bytes 2097152 | tf_op jit(solution)/shard_map/all_to_all | solution.py:27
  146.1 1.2 project.3
  147.3 8.9 %all_to_all.33.stats = f32[8,8,256]{2,1,0:T(8,128)S(1)} all-to-all(f32[8,8,256]{2,1,0:T(8,128)S(1)} %broadcast_in_dim.67), channel_id=1, replica_groups=mesh['zh'=4,'zl'=2,'yh'=4,'c'=2,'x'=4,'yl'=2] {'x','yl'}, dimensions={0} | all-to-all | bytes 131072 | tf_op jit(solution)/shard_map/all_to_all | solution.py:27
  (38 shorter events, 8.4 us)
Async XLA Ops:
  2.2 30.9 %copy-start.5 = (bf16[256]{0:T(256)(128)(2,1)S(1)}, bf16[256]{0:T(256)(128)(2,1)}, u32[]{:S(2)}) copy-start(bf16[256]{0:T(256)(128)(2,1)} %param.17) | copy-start | bytes 1540
  2.2 31.0 %copy-start.2 = (bf16[3,256]{1,0:T(4,128)(2,1)S(1)}, bf16[3,256]{1,0:T(4,128)(2,1)}, u32[]{:S(2)}) copy-start(bf16[3,256]{1,0:T(4,128)(2,1)} %param.15) | copy-start | bytes 4612
  2.2 17.1 %all-to-all-start = ((bf16[4,4,32,256]{3,2,1,0:T(8,128)(2,1)}), bf16[4,4,32,256]{3,2,1,0:T(8,128)(2,1)S(1)}, u32[]{:S(2)}, u32[]{:S(2)}) async-start(bf16[4,4,32,256]{3,2,1,0:T(8,128)(2,1)} %broadcast_in_dim.25), calls=%async_computation | async-start | bytes 524288 | tf_op jit(solution)/shard_map/all_to_all | solution.py:27
  12.8 34.8 %copy-start.3 = (s32[2]{0:T(128)S(1)}, s32[2]{0:T(128)}, u32[]{:S(2)}) copy-start(s32[2]{0:T(128)} %param.11) | copy-start | bytes 28
  12.8 34.8 %copy-start.4 = (s32[2]{0:T(128)S(1)}, s32[2]{0:T(128)}, u32[]{:S(2)}) copy-start(s32[2]{0:T(128)} %param.12) | copy-start | bytes 28
  20.4 35.8 %all-to-all-start.1 = ((bf16[4,4,4,32,256]{4,3,2,1,0:T(8,128)(2,1)}), bf16[4,4,4,32,256]{4,3,2,1,0:T(8,128)(2,1)S(1)}, u32[]{:S(2)}, u32[]{:S(2)}) async-start(bf16[4,4,4,32,256]{4,3,2,1,0:T(8,128)(2,1)} %broadcast_in_dim.29), calls=%async_computation.1 | async-start | bytes 2097152 | tf_op jit(solution)/shard_map/all_to_all | solution.py:27
  30.7 6.9 %collective-permute-start = (bf16[272,256]{1,0:T(8,128)(2,1)S(1)}, bf16[272,256]{1,0:T(8,128)(2,1)S(1)}, u32[]{:S(2)}, u32[]{:S(2)}) collective-permute-start(bf16[272,256]{1,0:T(8,128)(2,1)S(1)} %maximum_maximum_fusion), channel_id=1, source_target_pairs={{0,1},{1,0},{2,3},{3,2},{4,5},{5,4},{6,7},{7,6},{8,9},{9,8},{10,11... | collective-permute-start | bytes 417800 | tf_op jit(solution)/shard_map/ppermute | solution.py:244
  37.7 15.1 %collective-permute-start.3 = (bf16[2,272,256]{2,1,0:T(8,128)(2,1)S(1)}, bf16[2,272,256]{2,1,0:T(8,128)(2,1)S(1)}, u32[]{:S(2)}, u32[]{:S(2)}) collective-permute-start(bf16[2,272,256]{2,1,0:T(8,128)(2,1)S(1)} %pad_maximum_fusion.rest_4_), channel_id=1, source_target_pairs={{0,6},{2,4},{4,2},{6,0},{1,7},{3,5},{5,3},{7,1},{8,14},{10,12},{12... | collective-permute-start | bytes 835592 | tf_op jit(solution)/shard_map/ppermute | solution.py:246
  42.4 13.0 %collective-permute-start.2 = (bf16[2,272,256]{2,1,0:T(8,128)(2,1)S(1)}, bf16[2,272,256]{2,1,0:T(8,128)(2,1)S(1)}, u32[]{:S(2)}, u32[]{:S(2)}) collective-permute-start(bf16[2,272,256]{2,1,0:T(8,128)(2,1)S(1)} %pad_maximum_fusion.rest_4_), channel_id=1, source_target_pairs={{0,4},{2,6},{4,0},{6,2},{1,5},{3,7},{5,1},{7,3},{8,12},{10,14},{12... | collective-permute-start | bytes 835592 | tf_op jit(solution)/shard_map/ppermute | solution.py:246
  45.1 11.1 %collective-permute-start.1 = (bf16[2,272,256]{2,1,0:T(8,128)(2,1)S(1)}, bf16[2,272,256]{2,1,0:T(8,128)(2,1)S(1)}, u32[]{:S(2)}, u32[]{:S(2)}) collective-permute-start(bf16[2,272,256]{2,1,0:T(8,128)(2,1)S(1)} %pad_maximum_fusion.rest_4_), channel_id=1, source_target_pairs={{0,2},{2,0},{4,6},{6,4},{1,3},{3,1},{5,7},{7,5},{8,10},{10,8},{12,... | collective-permute-start | bytes 835592 | tf_op jit(solution)/shard_map/ppermute | solution.py:246
  56.2 25.1 %copy-start = (bf16[2,2,1024,256]{3,2,1,0:T(8,128)(2,1)S(1)}, bf16[2,2,1024,256]{3,2,1,0:T(8,128)(2,1)}, u32[]{:S(2)}) copy-start(bf16[2,2,1024,256]{3,2,1,0:T(8,128)(2,1)} %cache_ref.3) | copy-start | bytes 6291460
  56.3 17.0 %collective-permute-start.5 = (bf16[2,4,4,32,256]{4,3,2,1,0:T(8,128)(2,1)S(1)}, bf16[2,4,4,32,256]{4,3,2,1,0:T(8,128)(2,1)S(1)}, u32[]{:S(2)}, u32[]{:S(2)}) collective-permute-start(bf16[2,4,4,32,256]{4,3,2,1,0:T(8,128)(2,1)S(1)} %get-tuple-element.43), channel_id=1, source_target_pairs={{0,64},{64,128},{128,192},{192,256},{256,320},{320,384},{384,448},... | collective-permute-start | bytes 1572872 | tf_op jit(solution)/shard_map/ppermute | solution.py:251
  62.1 14.6 %collective-permute-start.6 = (bf16[2,4,4,32,256]{4,3,2,1,0:T(8,128)(2,1)S(1)}, bf16[2,4,4,32,256]{4,3,2,1,0:T(8,128)(2,1)S(1)}, u32[]{:S(2)}, u32[]{:S(2)}) collective-permute-start(bf16[2,4,4,32,256]{4,3,2,1,0:T(8,128)(2,1)S(1)} %get-tuple-element.42), channel_id=1, source_target_pairs={{0,448},{64,0},{128,64},{192,128},{256,192},{320,256},{384,320},{4... | collective-permute-start | bytes 1572872 | tf_op jit(solution)/shard_map/ppermute | solution.py:252
  64.4 14.2 %collective-permute-start.4 = (bf16[4,4,4,32,256]{4,3,2,1,0:T(8,128)(2,1)S(1)}, bf16[4,4,4,32,256]{4,3,2,1,0:T(8,128)(2,1)S(1)}, u32[]{:S(2)}, u32[]{:S(2)}) collective-permute-start(bf16[4,4,4,32,256]{4,3,2,1,0:T(8,128)(2,1)S(1)} %all-to-all-done.1.rest_0_), channel_id=1, source_target_pairs={{0,8},{8,0},{1,9},{9,1},{2,10},{10,2},{3,11},{11,3},{4,12},{12,4},... | collective-permute-start | bytes 3145736 | tf_op jit(solution)/shard_map/ppermute | solution.py:253
  76.7 4.6 %collective-permute-start.7 = (bf16[4,4,4,32,256]{4,3,2,1,0:T(8,128)(2,1)S(1)}, bf16[4,4,4,32,256]{4,3,2,1,0:T(8,128)(2,1)S(1)}, u32[]{:S(2)}, u32[]{:S(2)}) collective-permute-start(bf16[4,4,4,32,256]{4,3,2,1,0:T(8,128)(2,1)S(1)} %constant_dynamic-update-slice_fusion.rest_2_), channel_id=1, source_target_pairs={{0,8},{8,0},{1,9},{9,1},{2,10},{10,2},{3,11},{11,3},{4,12},{12,4},... | collective-permute-start | bytes 3145736 | tf_op jit(solution)/shard_map/ppermute | solution.py:255
  85.2 20.2 %copy-start.1 = (bf16[256,256]{1,0:T(8,128)(2,1)S(1)}, bf16[256,256]{1,0:T(8,128)(2,1)}, u32[]{:S(2)}) copy-start(bf16[256,256]{1,0:T(8,128)(2,1)} %res_ref.1) | copy-start | bytes 393220

commit v3 on v2

--- a/solution.py
+++ b/solution.py
@@ -50,18 +50,17 @@
 
 def attention_kernel(layer, info, starts, stops, params, cache_ref, prev, *rest):
     pieces, rest = rest[:4], rest[4:]
-    count = 4 if layer == 0 else 2
+    count = 2 if layer == 0 else 3
     inputs, rest = rest[:count], rest[count:]
-    att_ref, new_ref, extra_ref, new, cache, sems, x = rest
+    att_ref, new_ref = rest[:2]
+    new, cache, sems, x = rest[-4:]
     fetch = pltpu.make_async_copy(cache_ref.at[layer], cache, sems.at[2])
     fetch.start()
     if layer == 0:
         for k in range(8):
-            source = info[2] ^ k
-            x[source] = inputs[k // 2][k % 2, 0:256, :]
-            extra_ref[source] = inputs[k // 2][k % 2, 256:272, :]
+            x[info[2] ^ k] = inputs[k % 2][k // 2, 0:256, :]
     else:
-        x_ref, gs_ref = inputs
+        x_ref = inputs[0]
         total = jnp.zeros((256, 1), F32)
         for n in range(8):
             total += jnp.sum(x_ref[n].astype(F32), axis=1, keepdims=True)
@@ -71,11 +70,12 @@
             centered = x_ref[n].astype(F32) - mean
             spread_sum += jnp.sum(centered * centered, axis=1, keepdims=True)
         scale = lax.rsqrt(spread_sum / 2048.0 + EPSILON)
-        for n in range(8):
-            both = gs_ref[n].astype(F32)
-            normed = (x_ref[n].astype(F32) - mean) * scale * both[0:1] + both[1:2]
-            x[n] = normed.astype(BF16)
-        extra_ref[...] = x[info[2]]
+        for k in range(8):
+            source = info[2] ^ k
+            both = inputs[1 + k % 2][k // 2, 256:272, :].astype(F32)
+            normed = (x_ref[source].astype(F32) - mean) * scale * both[0:1] + both[1:2]
+            x[source] = normed.astype(BF16)
+        rest[2][...] = x[info[2]]
     bias = params[...]
     parts = []
     copies = []
@@ -91,7 +91,7 @@
             copies.append(copy)
     q, k_new, v_new = parts
     fetch.wait()
-    factor = 1.0 / math.sqrt(HEAD)
+    factor = math.log2(math.e) / math.sqrt(HEAD)
     column = lax.broadcasted_iota(jnp.int32, (1, 1024), 1)
     causal = lax.broadcasted_iota(jnp.int32, (SPAN, SPAN), 0) >= lax.broadcasted_iota(
         jnp.int32, (SPAN, SPAN), 1
@@ -107,8 +107,8 @@
             top = jnp.maximum(
                 jnp.max(sc, axis=1, keepdims=True), jnp.max(sn, axis=1, keepdims=True)
             )
-            pc = jnp.exp(sc - top)
-            pn = jnp.exp(sn - top)
+            pc = jnp.exp2(sc - top)
+            pn = jnp.exp2(sn - top)
             norm = jnp.sum(pc, axis=1, keepdims=True) + jnp.sum(pn, axis=1, keepdims=True)
             out = dot(pc.astype(BF16), cache[1, :, cols]) + dot(
                 pn.astype(BF16), v_new[rows, cols]
@@ -123,17 +123,16 @@
     vmem = pl.BlockSpec(memory_space=pltpu.VMEM)
     anywhere = pl.BlockSpec(memory_space=pl.ANY)
     tile = jax.ShapeDtypeStruct((256, 256), BF16)
-    vectors = jax.ShapeDtypeStruct((8, 16, 256), BF16)
-    out_shape = [
-        tile,
-        jax.ShapeDtypeStruct((2, 2, 256, 256), BF16),
-        vectors if layer == 0 else tile,
-    ]
+    out_shape = [tile, jax.ShapeDtypeStruct((2, 2, 256, 256), BF16)]
+    out_specs = [vmem, anywhere]
+    if layer > 0:
+        out_shape.append(tile)
+        out_specs.append(vmem)
     return pl.pallas_call(
         functools.partial(attention_kernel, layer),
         out_shape=out_shape,
         in_specs=[smem] * 3 + [vmem, anywhere, anywhere] + [vmem] * (4 + len(inputs)),
-        out_specs=[vmem, anywhere, vmem],
+        out_specs=out_specs,
         scratch_shapes=[
             pltpu.VMEM((2, 256, 256), BF16),
             pltpu.VMEM((2, 1024, 256), BF16),
@@ -233,36 +232,36 @@
     stops = starts + cache_lengths
     vectors = [qkv_bias, out_bias[None], norm_gain[None], norm_shift[None]]
     params = jnp.pad(jnp.concatenate(vectors, axis=0).astype(F32), ((0, 2), (0, 0)))
+
+    pieces = jnp.concatenate([w_qkv.transpose(1, 0, 2), w_out[None]], axis=0)
     payload = jnp.concatenate(
         [hidden_in, norm_gain[None], norm_shift[None], jnp.zeros((14, 256), BF16)], axis=0
     )
-
-    pieces = jnp.concatenate([w_qkv.transpose(1, 0, 2), w_out[None]], axis=0)
-    near = spread(pieces, "yh", 4)
-    near, payload = lax.optimization_barrier((near, payload))
-    same = spread(near, "zh", 4)
-    blocks = jnp.stack([payload, lax.ppermute(payload, "yl", SWAP)])
-    blocks = [blocks] + [
-        lax.ppermute(blocks, "x", [(i, i ^ k) for i in range(4)]) for k in range(1, 4)
-    ]
-    same, blocks, params, info, starts, stops = lax.optimization_barrier(
-        (same, blocks, params, info, starts, stops)
+    mine = jnp.stack(
+        [payload]
+        + [lax.ppermute(payload, "x", [(i, i ^ k) for i in range(4)]) for k in range(1, 4)]
+    )
+    same = spread(pieces, ("zh", "yh"), 16).reshape(4, 4, 4, 32, 256)
+    same, mine, params, info, starts, stops = lax.optimization_barrier(
+        (same, mine, params, info, starts, stops)
     )
     left = lax.ppermute(same[:2], ("zh", "zl"), [(i, (i + 1) % 8) for i in range(8)])
     right = lax.ppermute(same[2:], ("zh", "zl"), [(i, (i - 1) % 8) for i in range(8)])
     same_swap = lax.ppermute(same, "c", SWAP)
+    blocks = [mine, lax.ppermute(mine, "yl", SWAP)]
+    left, right, blocks = lax.optimization_barrier((left, right, blocks))
     away = jnp.concatenate([left, right], axis=0)
     pieces = [same, same_swap, away, lax.ppermute(away, "c", SWAP)]
 
     blank = jnp.zeros((8, 128), BF16)
-    att, new_cache, vectors = attention(
+    att, new_cache = attention(
         0, info, starts, stops, params, cache_kv, blank, pieces, blocks
     )
     heads = spread(att, NARROW, 8)
     (summed,) = project(False, info, heads, params, hidden_in, pieces)
     rows = spread(summed, NARROW, 8)
     att, new_cache, carried = attention(
-        1, info, starts, stops, params, cache_kv, new_cache, pieces, [rows, vectors]
+        1, info, starts, stops, params, cache_kv, new_cache, pieces, [rows] + blocks
     )
     heads = spread(att, NARROW, 8)
     summed, stats = project(True, info, heads, params, carried, pieces)

time: 158 us -> 155 us (0.981)
  the two profiles are of different devices: /device:TPU:16 before, /device:TPU:56 now
where the time goes in v3:
time: 155 us; the launch traced here: 154 us
  blocking collectives  63.9 us (41%)
  starting transfers between devices  43.2 us (28%)
  waiting for transfers between devices  31.3 us (20%)
  Pallas kernels  12.1 us (8%)
  local copies, waits for them, and re-layouts  1.63 us (1%)
    all_to_all x4, blocking collectives, spread(): lax.all_to_all(jnp.broadcast_to(x[None], (count,) + x.shape), axes, 0, 0,...  63.9 us
    all_to_all x1, starting transfers between devices, spread(): lax.all_to_all(jnp.broadcast_to(x[None], (count,) + x.shape), axes, 0, 0,...  15.5 us
    all_to_all x1, waiting for transfers between devices, spread(): lax.all_to_all(jnp.broadcast_to(x[None], (count,) + x.shape), axes, 0, 0,...  13.4 us
    ppermute x3, starting transfers between devices, shards(): lax.ppermute(payload, 'x', [(i, i ^ k) for i in range(4)])  9.9 us
    pallas_call x2, Pallas kernels, attention(): pl.pallas_call(functools.partial(attention_kernel, layer), out_shape=out_...  8.97 us
    ppermute x1, starting transfers between devices, shards(): blocks = [mine, lax.ppermute(mine, 'yl', SWAP)]  8.11 us
    ppermute x1, waiting for transfers between devices, shards(): lax.ppermute(same[2:], ('zh', 'zl'), [(i, (i - 1) % 8) for i in range(8)])  6.83 us
    ppermute x3, waiting for transfers between devices, shards(): lax.ppermute(payload, 'x', [(i, i ^ k) for i in range(4)])  5.4 us
  transfers between devices with their start and end apart: 9, of which 6 were waited for; matrix products, arithmetic and copies ran while one was open for 0% of the time, Pallas kernels for 0%

profile of v3, /device:TPU:56, one launch (start us, length us, event | category | flops | bytes accessed | tf_op | source)
XLA Modules:
  0.0 154.4 jit_solution(3281304231851623739)
XLA Ops:
  1.6 1.1 broadcast_in_dim.23
  2.7 15.5 %all-to-all-start = ((bf16[16,4,32,256]{3,2,1,0:T(8,128)(2,1)}), bf16[16,4,32,256]{3,2,1,0:T(8,128)(2,1)S(1)}, u32[]{:S(2)}, u32[]{:S(2)}) async-start(bf16[16,4,32,256]{3,2,1,0:T(8,128)(2,1)} %broadcast_in_dim.23), calls=%async_computation | async-start | bytes 2097152 | tf_op jit(solution)/shard_map/all_to_all | solution.py:27
  18.4 4.9 %collective-permute-start.1 = (bf16[272,256]{1,0:T(8,128)(2,1)S(1)}, bf16[272,256]{1,0:T(8,128)(2,1)S(1)}, u32[]{:S(2)}, u32[]{:S(2)}) collective-permute-start(bf16[272,256]{1,0:T(8,128)(2,1)S(1)} %maximum_maximum_fusion), channel_id=1, source_target_pairs={{0,4},{2,6},{4,0},{6,2},{1,5},{3,7},{5,1},{7,3},{8,12},{10,14},{12... | collective-permute-start | bytes 417800 | tf_op jit(solution)/shard_map/ppermute | solution.py:242
  23.4 2.5 %collective-permute-start = (bf16[272,256]{1,0:T(8,128)(2,1)S(1)}, bf16[272,256]{1,0:T(8,128)(2,1)S(1)}, u32[]{:S(2)}, u32[]{:S(2)}) collective-permute-start(bf16[272,256]{1,0:T(8,128)(2,1)S(1)} %maximum_maximum_fusion), channel_id=1, source_target_pairs={{0,2},{2,0},{4,6},{6,4},{1,3},{3,1},{5,7},{7,5},{8,10},{10,8},{12,... | collective-permute-start | bytes 417800 | tf_op jit(solution)/shard_map/ppermute | solution.py:242
  25.9 2.5 %collective-permute-start.2 = (bf16[272,256]{1,0:T(8,128)(2,1)S(1)}, bf16[272,256]{1,0:T(8,128)(2,1)S(1)}, u32[]{:S(2)}, u32[]{:S(2)}) collective-permute-start(bf16[272,256]{1,0:T(8,128)(2,1)S(1)} %maximum_maximum_fusion), channel_id=1, source_target_pairs={{0,6},{2,4},{4,2},{6,0},{1,7},{3,5},{5,3},{7,1},{8,14},{10,12},{12... | collective-permute-start | bytes 417800 | tf_op jit(solution)/shard_map/ppermute | solution.py:242
  28.6 1.7 %collective-permute-done = bf16[272,256]{1,0:T(8,128)(2,1)S(1)} collective-permute-done((bf16[272,256]{1,0:T(8,128)(2,1)S(1)}, bf16[272,256]{1,0:T(8,128)(2,1)S(1)}, u32[]{:S(2)}, u32[]{:S(2)}) %collective-permute-start) | collective-permute-done | bytes 139296 | tf_op jit(solution)/shard_map/ppermute | solution.py:242
  30.3 3.7 %collective-permute-done.2 = bf16[272,256]{1,0:T(8,128)(2,1)S(1)} collective-permute-done((bf16[272,256]{1,0:T(8,128)(2,1)S(1)}, bf16[272,256]{1,0:T(8,128)(2,1)S(1)}, u32[]{:S(2)}, u32[]{:S(2)}) %collective-permute-start.2) | collective-permute-done | bytes 139296 | tf_op jit(solution)/shard_map/ppermute | solution.py:242
  34.1 13.4 %all-to-all-done = bf16[16,4,32,256]{3,2,1,0:T(8,128)(2,1)S(1)} async-done(((bf16[16,4,32,256]{3,2,1,0:T(8,128)(2,1)}), bf16[16,4,32,256]{3,2,1,0:T(8,128)(2,1)S(1)}, u32[]{:S(2)}, u32[]{:S(2)}) %all-to-all-start) | async-done | bytes 1048608 | tf_op jit(solution)/shard_map/all_to_all | solution.py:27
  47.5 8.1 %collective-permute-start.6 = (bf16[4,272,256]{2,1,0:T(8,128)(2,1)S(1)}, bf16[4,272,256]{2,1,0:T(8,128)(2,1)S(1)}, u32[]{:S(2)}, u32[]{:S(2)}) collective-permute-start(bf16[4,272,256]{2,1,0:T(8,128)(2,1)S(1)} %pad_maximum_fusion.rest_4_.rest_5_), channel_id=1, source_target_pairs={{0,1},{1,0},{2,3},{3,2},{4,5},{5,4},{6,7},{7,6},{8,9},{9,8},{10,11... | collective-permute-start | bytes 1671176 | tf_op jit(solution)/shard_map/ppermute | solution.py:251
  55.7 3.7 %collective-permute-start.5 = (bf16[2,4,4,32,256]{4,3,2,1,0:T(8,128)(2,1)S(1)}, bf16[2,4,4,32,256]{4,3,2,1,0:T(8,128)(2,1)S(1)}, u32[]{:S(2)}, u32[]{:S(2)}) collective-permute-start(bf16[2,4,4,32,256]{4,3,2,1,0:T(8,128)(2,1)S(1)} %get-tuple-element.38), channel_id=1, source_target_pairs={{0,448},{64,0},{128,64},{192,128},{256,192},{320,256},{384,320},{4... | collective-permute-start | bytes 1572872 | tf_op jit(solution)/shard_map/ppermute | solution.py:249
  59.5 2.1 %collective-permute-start.4 = (bf16[2,4,4,32,256]{4,3,2,1,0:T(8,128)(2,1)S(1)}, bf16[2,4,4,32,256]{4,3,2,1,0:T(8,128)(2,1)S(1)}, u32[]{:S(2)}, u32[]{:S(2)}) collective-permute-start(bf16[2,4,4,32,256]{4,3,2,1,0:T(8,128)(2,1)S(1)} %get-tuple-element.39), channel_id=1, source_target_pairs={{0,64},{64,128},{128,192},{192,256},{256,320},{320,384},{384,448},... | collective-permute-start | bytes 1572872 | tf_op jit(solution)/shard_map/ppermute | solution.py:248
  61.6 1.9 %collective-permute-start.3 = (bf16[4,4,4,32,256]{4,3,2,1,0:T(8,128)(2,1)S(1)}, bf16[4,4,4,32,256]{4,3,2,1,0:T(8,128)(2,1)S(1)}, u32[]{:S(2)}, u32[]{:S(2)}) collective-permute-start(bf16[4,4,4,32,256]{4,3,2,1,0:T(8,128)(2,1)S(1)} %bitcast.12), channel_id=1, source_target_pairs={{0,8},{8,0},{1,9},{9,1},{2,10},{10,2},{3,11},{11,3},{4,12},{12,4},... | collective-permute-start | bytes 3145736 | tf_op jit(solution)/shard_map/ppermute | solution.py:250
  63.5 6.8 %collective-permute-done.5 = bf16[2,4,4,32,256]{4,3,2,1,0:T(8,128)(2,1)S(1)} collective-permute-done((bf16[2,4,4,32,256]{4,3,2,1,0:T(8,128)(2,1)S(1)}, bf16[2,4,4,32,256]{4,3,2,1,0:T(8,128)(2,1)S(1)}, u32[]{:S(2)}, u32[]{:S(2)}) %collective-permute-start.5) | collective-permute-done | bytes 524320 | tf_op jit(solution)/shard_map/ppermute | solution.py:249
  70.3 3.1 %collective-permute-done.4 = bf16[2,4,4,32,256]{4,3,2,1,0:T(8,128)(2,1)S(1)} collective-permute-done((bf16[2,4,4,32,256]{4,3,2,1,0:T(8,128)(2,1)S(1)}, bf16[2,4,4,32,256]{4,3,2,1,0:T(8,128)(2,1)S(1)}, u32[]{:S(2)}, u32[]{:S(2)}) %collective-permute-start.4) | collective-permute-done | bytes 524320 | tf_op jit(solution)/shard_map/ppermute | solution.py:248
  73.5 1.9 %collective-permute-start.7 = (bf16[4,4,4,32,256]{4,3,2,1,0:T(8,128)(2,1)S(1)}, bf16[4,4,4,32,256]{4,3,2,1,0:T(8,128)(2,1)S(1)}, u32[]{:S(2)}, u32[]{:S(2)}) collective-permute-start(bf16[4,4,4,32,256]{4,3,2,1,0:T(8,128)(2,1)S(1)} %constant_dynamic-update-slice_fusion.rest_2_), channel_id=1, source_target_pairs={{0,8},{8,0},{1,9},{9,1},{2,10},{10,2},{3,11},{11,3},{4,12},{12,4},... | collective-permute-start | bytes 3145736 | tf_op jit(solution)/shard_map/ppermute | solution.py:254
  75.5 2.6 %collective-permute-done.7.rest_3_ = bf16[4,4,4,32,256]{4,3,2,1,0:T(8,128)(2,1)S(1)} collective-permute-done((bf16[4,4,4,32,256]{4,3,2,1,0:T(8,128)(2,1)S(1)}, bf16[4,4,4,32,256]{4,3,2,1,0:T(8,128)(2,1)S(1)}, u32[]{:S(2)}, u32[]{:S(2)}) %collective-permute-start.7) | collective-permute-done | bytes 1048608 | tf_op jit(solution)/shard_map/ppermute | solution.py:254
  78.1 3.9 %attention.2 = (bf16[256,256]{1,0:T(8,128)(2,1)S(1)}, bf16[2,2,256,256]{3,2,1,0:T(8,128)(2,1)}) custom-call(s32[3]{0:T(128)S(1)} %pad_add_fusion.info, s32[2]{0:T(128)S(1)} %get-tuple-element.20.starts, s32[2]{0:T(128)S(1)} %get-tuple-element.21.stops, f32[8,256]{1,0:T(8,128)S(1)} %fusion.7.params, bf16[2,2,1024,256]{3,2,1,0:T(8,128)(2,1)S(1)} %copy-done, ...), custom_call_target="tpu_custom_call" | custom-call | flops 1107296256 | bytes 6291456 | tf_op jit(solution)/shard_map/attention/pallas_call | solution.py:131
  82.1 20.4 %all_to_all.25.att = bf16[8,256,256]{2,1,0:T(8,128)(2,1)S(1)} all-to-all(bf16[8,256,256]{2,1,0:T(8,128)(2,1)S(1)} %broadcast_in_dim.57), channel_id=1, replica_groups=mesh['zh'=4,'zl'=2,'yh'=4,'c'=2,'x'=4,'yl'=2] {'x','yl'}, dimensions={0} | all-to-all | bytes 2097152 | tf_op jit(solution)/shard_map/all_to_all | solution.py:27
  102.4 1.0 project.2
  103.5 17.7 %all_to_all.26.rest_4_ = bf16[8,256,256]{2,1,0:T(8,128)(2,1)S(1)} all-to-all(bf16[8,256,256]{2,1,0:T(8,128)(2,1)S(1)} %broadcast_in_dim.58), channel_id=1, replica_groups=mesh['zh'=4,'zl'=2,'yh'=4,'c'=2,'x'=4,'yl'=2] {'x','yl'}, dimensions={0} | all-to-all | bytes 2097152 | tf_op jit(solution)/shard_map/all_to_all | solution.py:27
  121.3 5.1 %attention.3 = (bf16[256,256]{1,0:T(8,128)(2,1)S(1)}, bf16[2,2,256,256]{3,2,1,0:T(8,128)(2,1)}, bf16[256,256]{1,0:T(8,128)(2,1)S(1)}) custom-call(s32[3]{0:T(128)S(1)} %pad_add_fusion.info, s32[2]{0:T(128)S(1)} %get-tuple-element.20.starts, s32[2]{0:T(128)S(1)} %get-tuple-element.21.stops, ...), custom_call_target="tpu_custom_call", output_to_operand_aliasing={{1}: (5, {})} | custom-call | flops 1107296256 | bytes 6291456 | tf_op jit(solution)/shard_map/attention/pallas_call | solution.py:131
  126.5 16.9 %all_to_all.27.att = bf16[8,256,256]{2,1,0:T(8,128)(2,1)S(1)} all-to-all(bf16[8,256,256]{2,1,0:T(8,128)(2,1)S(1)} %broadcast_in_dim.59), channel_id=1, replica_groups=mesh['zh'=4,'zl'=2,'yh'=4,'c'=2,'x'=4,'yl'=2] {'x','yl'}, dimensions={0} | all-to-all | bytes 2097152 | tf_op jit(solution)/shard_map/all_to_all | solution.py:27
  143.3 1.2 project.3
  144.6 8.9 %all_to_all.28.stats = f32[8,8,256]{2,1,0:T(8,128)S(1)} all-to-all(f32[8,8,256]{2,1,0:T(8,128)S(1)} %broadcast_in_dim.60), channel_id=1, replica_groups=mesh['zh'=4,'zl'=2,'yh'=4,'c'=2,'x'=4,'yl'=2] {'x','yl'}, dimensions={0} | all-to-all | bytes 131072 | tf_op jit(solution)/shard_map/all_to_all | solution.py:27
  (40 shorter events, 2.7 us)
Async XLA Ops:
  0.6 17.6 %copy-start.5 = (bf16[256]{0:T(256)(128)(2,1)S(1)}, bf16[256]{0:T(256)(128)(2,1)}, u32[]{:S(2)}) copy-start(bf16[256]{0:T(256)(128)(2,1)} %param.18) | copy-start | bytes 1540
  0.6 17.6 %copy-start.6 = (bf16[256]{0:T(256)(128)(2,1)S(1)}, bf16[256]{0:T(256)(128)(2,1)}, u32[]{:S(2)}) copy-start(bf16[256]{0:T(256)(128)(2,1)} %param.19) | copy-start | bytes 1540
  0.7 17.7 %copy-start.1 = (bf16[256,256]{1,0:T(8,128)(2,1)S(1)}, bf16[256,256]{1,0:T(8,128)(2,1)}, u32[]{:S(2)}) copy-start(bf16[256,256]{1,0:T(8,128)(2,1)} %res_ref.1) | copy-start | bytes 393220
  0.7 27.7 %copy-start.4 = (s32[2]{0:T(128)S(1)}, s32[2]{0:T(128)}, u32[]{:S(2)}) copy-start(s32[2]{0:T(128)} %param.12) | copy-start | bytes 28
  0.7 27.7 %copy-start.3 = (s32[2]{0:T(128)S(1)}, s32[2]{0:T(128)}, u32[]{:S(2)}) copy-start(s32[2]{0:T(128)} %param.11) | copy-start | bytes 28
  0.7 27.9 %copy-start.7 = (bf16[256]{0:T(256)(128)(2,1)S(1)}, bf16[256]{0:T(256)(128)(2,1)}, u32[]{:S(2)}) copy-start(bf16[256]{0:T(256)(128)(2,1)} %param.17) | copy-start | bytes 1540
  0.7 27.9 %copy-start.2 = (bf16[3,256]{1,0:T(4,128)(2,1)S(1)}, bf16[3,256]{1,0:T(4,128)(2,1)}, u32[]{:S(2)}) copy-start(bf16[3,256]{1,0:T(4,128)(2,1)} %param.15) | copy-start | bytes 4612
  2.7 44.8 %all-to-all-start = ((bf16[16,4,32,256]{3,2,1,0:T(8,128)(2,1)}), bf16[16,4,32,256]{3,2,1,0:T(8,128)(2,1)S(1)}, u32[]{:S(2)}, u32[]{:S(2)}) async-start(bf16[16,4,32,256]{3,2,1,0:T(8,128)(2,1)} %broadcast_in_dim.23), calls=%async_computation | async-start | bytes 2097152 | tf_op jit(solution)/shard_map/all_to_all | solution.py:27
  18.4 10.2 %collective-permute-start.1 = (bf16[272,256]{1,0:T(8,128)(2,1)S(1)}, bf16[272,256]{1,0:T(8,128)(2,1)S(1)}, u32[]{:S(2)}, u32[]{:S(2)}) collective-permute-start(bf16[272,256]{1,0:T(8,128)(2,1)S(1)} %maximum_maximum_fusion), channel_id=1, source_target_pairs={{0,4},{2,6},{4,0},{6,2},{1,5},{3,7},{5,1},{7,3},{8,12},{10,14},{12... | collective-permute-start | bytes 417800 | tf_op jit(solution)/shard_map/ppermute | solution.py:242
  23.4 6.9 %collective-permute-start = (bf16[272,256]{1,0:T(8,128)(2,1)S(1)}, bf16[272,256]{1,0:T(8,128)(2,1)S(1)}, u32[]{:S(2)}, u32[]{:S(2)}) collective-permute-start(bf16[272,256]{1,0:T(8,128)(2,1)S(1)} %maximum_maximum_fusion), channel_id=1, source_target_pairs={{0,2},{2,0},{4,6},{6,4},{1,3},{3,1},{5,7},{7,5},{8,10},{10,8},{12,... | collective-permute-start | bytes 417800 | tf_op jit(solution)/shard_map/ppermute | solution.py:242
  25.9 8.2 %collective-permute-start.2 = (bf16[272,256]{1,0:T(8,128)(2,1)S(1)}, bf16[272,256]{1,0:T(8,128)(2,1)S(1)}, u32[]{:S(2)}, u32[]{:S(2)}) collective-permute-start(bf16[272,256]{1,0:T(8,128)(2,1)S(1)} %maximum_maximum_fusion), channel_id=1, source_target_pairs={{0,6},{2,4},{4,2},{6,0},{1,7},{3,5},{5,3},{7,1},{8,14},{10,12},{12... | collective-permute-start | bytes 417800 | tf_op jit(solution)/shard_map/ppermute | solution.py:242
  47.5 30.6 %copy-start = (bf16[2,2,1024,256]{3,2,1,0:T(8,128)(2,1)S(1)}, bf16[2,2,1024,256]{3,2,1,0:T(8,128)(2,1)}, u32[]{:S(2)}) copy-start(bf16[2,2,1024,256]{3,2,1,0:T(8,128)(2,1)} %cache_ref.3) | copy-start | bytes 6291460
  47.5 25.9 %collective-permute-start.6 = (bf16[4,272,256]{2,1,0:T(8,128)(2,1)S(1)}, bf16[4,272,256]{2,1,0:T(8,128)(2,1)S(1)}, u32[]{:S(2)}, u32[]{:S(2)}) collective-permute-start(bf16[4,272,256]{2,1,0:T(8,128)(2,1)S(1)} %pad_maximum_fusion.rest_4_.rest_5_), channel_id=1, source_target_pairs={{0,1},{1,0},{2,3},{3,2},{4,5},{5,4},{6,7},{7,6},{8,9},{9,8},{10,11... | collective-permute-start | bytes 1671176 | tf_op jit(solution)/shard_map/ppermute | solution.py:251
  55.7 14.6 %collective-permute-start.5 = (bf16[2,4,4,32,256]{4,3,2,1,0:T(8,128)(2,1)S(1)}, bf16[2,4,4,32,256]{4,3,2,1,0:T(8,128)(2,1)S(1)}, u32[]{:S(2)}, u32[]{:S(2)}) collective-permute-start(bf16[2,4,4,32,256]{4,3,2,1,0:T(8,128)(2,1)S(1)} %get-tuple-element.38), channel_id=1, source_target_pairs={{0,448},{64,0},{128,64},{192,128},{256,192},{320,256},{384,320},{4... | collective-permute-start | bytes 1572872 | tf_op jit(solution)/shard_map/ppermute | solution.py:249
  59.5 14.0 %collective-permute-start.4 = (bf16[2,4,4,32,256]{4,3,2,1,0:T(8,128)(2,1)S(1)}, bf16[2,4,4,32,256]{4,3,2,1,0:T(8,128)(2,1)S(1)}, u32[]{:S(2)}, u32[]{:S(2)}) collective-permute-start(bf16[2,4,4,32,256]{4,3,2,1,0:T(8,128)(2,1)S(1)} %get-tuple-element.39), channel_id=1, source_target_pairs={{0,64},{64,128},{128,192},{192,256},{256,320},{320,384},{384,448},... | collective-permute-start | bytes 1572872 | tf_op jit(solution)/shard_map/ppermute | solution.py:248
  61.6 13.9 %collective-permute-start.3 = (bf16[4,4,4,32,256]{4,3,2,1,0:T(8,128)(2,1)S(1)}, bf16[4,4,4,32,256]{4,3,2,1,0:T(8,128)(2,1)S(1)}, u32[]{:S(2)}, u32[]{:S(2)}) collective-permute-start(bf16[4,4,4,32,256]{4,3,2,1,0:T(8,128)(2,1)S(1)} %bitcast.12), channel_id=1, source_target_pairs={{0,8},{8,0},{1,9},{9,1},{2,10},{10,2},{3,11},{11,3},{4,12},{12,4},... | collective-permute-start | bytes 3145736 | tf_op jit(solution)/shard_map/ppermute | solution.py:250
  73.5 4.6 %collective-permute-start.7 = (bf16[4,4,4,32,256]{4,3,2,1,0:T(8,128)(2,1)S(1)}, bf16[4,4,4,32,256]{4,3,2,1,0:T(8,128)(2,1)S(1)}, u32[]{:S(2)}, u32[]{:S(2)}) collective-permute-start(bf16[4,4,4,32,256]{4,3,2,1,0:T(8,128)(2,1)S(1)} %constant_dynamic-update-slice_fusion.rest_2_), channel_id=1, source_target_pairs={{0,8},{8,0},{1,9},{9,1},{2,10},{10,2},{3,11},{11,3},{4,12},{12,4},... | collective-permute-start | bytes 3145736 | tf_op jit(solution)/shard_map/ppermute | solution.py:254

commit v4 on v3

--- a/solution.py
+++ b/solution.py
@@ -61,14 +61,15 @@
             x[info[2] ^ k] = inputs[k % 2][k // 2, 0:256, :]
     else:
         x_ref = inputs[0]
-        total = jnp.zeros((256, 1), F32)
+        total = jnp.zeros((256, 256), F32)
         for n in range(8):
-            total += jnp.sum(x_ref[n].astype(F32), axis=1, keepdims=True)
-        mean = total / 2048.0
-        spread_sum = jnp.zeros((256, 1), F32)
+            total += x_ref[n].astype(F32)
+        mean = jnp.sum(total, axis=1, keepdims=True) / 2048.0
+        squares = jnp.zeros((256, 256), F32)
         for n in range(8):
             centered = x_ref[n].astype(F32) - mean
-            spread_sum += jnp.sum(centered * centered, axis=1, keepdims=True)
+            squares += centered * centered
+        spread_sum = jnp.sum(squares, axis=1, keepdims=True)
         scale = lax.rsqrt(spread_sum / 2048.0 + EPSILON)
         for k in range(8):
             source = info[2] ^ k

time: 155 us -> 155 us (level)
  no operation moved by 1% of the time
where the time goes in v4:
time: 155 us; the launch traced here: 154 us
  blocking collectives  63.9 us (41%)
  starting transfers between devices  43.2 us (28%)
  waiting for transfers between devices  31.3 us (20%)
  Pallas kernels  11.9 us (8%)
  local copies, waits for them, and re-layouts  1.63 us (1%)
    all_to_all x4, blocking collectives, spread(): lax.all_to_all(jnp.broadcast_to(x[None], (count,) + x.shape), axes, 0, 0,...  63.9 us
    all_to_all x1, starting transfers between devices, spread(): lax.all_to_all(jnp.broadcast_to(x[None], (count,) + x.shape), axes, 0, 0,...  15.5 us
    all_to_all x1, waiting for transfers between devices, spread(): lax.all_to_all(jnp.broadcast_to(x[None], (count,) + x.shape), axes, 0, 0,...  13.4 us
    ppermute x3, starting transfers between devices, shards(): lax.ppermute(payload, 'x', [(i, i ^ k) for i in range(4)])  9.9 us
    pallas_call x2, Pallas kernels, attention(): pl.pallas_call(functools.partial(attention_kernel, layer), out_shape=out_...  8.76 us
    ppermute x1, starting transfers between devices, shards(): blocks = [mine, lax.ppermute(mine, 'yl', SWAP)]  8.11 us
    ppermute x1, waiting for transfers between devices, shards(): lax.ppermute(same[2:], ('zh', 'zl'), [(i, (i - 1) % 8) for i in range(8)])  6.83 us
    ppermute x3, waiting for transfers between devices, shards(): lax.ppermute(payload, 'x', [(i, i ^ k) for i in range(4)])  5.4 us
  transfers between devices with their start and end apart: 9, of which 6 were waited for; matrix products, arithmetic and copies ran while one was open for 0% of the time, Pallas kernels for 0%

profile of v4, /device:TPU:56, one launch (start us, length us, event | category | flops | bytes accessed | tf_op | source)
XLA Modules:
  0.0 154.2 jit_solution(492120635715289710)
XLA Ops:
  1.6 1.1 broadcast_in_dim.23
  2.7 15.5 %all-to-all-start = ((bf16[16,4,32,256]{3,2,1,0:T(8,128)(2,1)}), bf16[16,4,32,256]{3,2,1,0:T(8,128)(2,1)S(1)}, u32[]{:S(2)}, u32[]{:S(2)}) async-start(bf16[16,4,32,256]{3,2,1,0:T(8,128)(2,1)} %broadcast_in_dim.23), calls=%async_computation | async-start | bytes 2097152 | tf_op jit(solution)/shard_map/all_to_all | solution.py:27
  18.4 4.9 %collective-permute-start.1 = (bf16[272,256]{1,0:T(8,128)(2,1)S(1)}, bf16[272,256]{1,0:T(8,128)(2,1)S(1)}, u32[]{:S(2)}, u32[]{:S(2)}) collective-permute-start(bf16[272,256]{1,0:T(8,128)(2,1)S(1)} %maximum_maximum_fusion), channel_id=1, source_target_pairs={{0,4},{2,6},{4,0},{6,2},{1,5},{3,7},{5,1},{7,3},{8,12},{10,14},{12... | collective-permute-start | bytes 417800 | tf_op jit(solution)/shard_map/ppermute | solution.py:243
  23.4 2.5 %collective-permute-start = (bf16[272,256]{1,0:T(8,128)(2,1)S(1)}, bf16[272,256]{1,0:T(8,128)(2,1)S(1)}, u32[]{:S(2)}, u32[]{:S(2)}) collective-permute-start(bf16[272,256]{1,0:T(8,128)(2,1)S(1)} %maximum_maximum_fusion), channel_id=1, source_target_pairs={{0,2},{2,0},{4,6},{6,4},{1,3},{3,1},{5,7},{7,5},{8,10},{10,8},{12,... | collective-permute-start | bytes 417800 | tf_op jit(solution)/shard_map/ppermute | solution.py:243
  25.9 2.5 %collective-permute-start.2 = (bf16[272,256]{1,0:T(8,128)(2,1)S(1)}, bf16[272,256]{1,0:T(8,128)(2,1)S(1)}, u32[]{:S(2)}, u32[]{:S(2)}) collective-permute-start(bf16[272,256]{1,0:T(8,128)(2,1)S(1)} %maximum_maximum_fusion), channel_id=1, source_target_pairs={{0,6},{2,4},{4,2},{6,0},{1,7},{3,5},{5,3},{7,1},{8,14},{10,12},{12... | collective-permute-start | bytes 417800 | tf_op jit(solution)/shard_map/ppermute | solution.py:243
  28.6 1.7 %collective-permute-done = bf16[272,256]{1,0:T(8,128)(2,1)S(1)} collective-permute-done((bf16[272,256]{1,0:T(8,128)(2,1)S(1)}, bf16[272,256]{1,0:T(8,128)(2,1)S(1)}, u32[]{:S(2)}, u32[]{:S(2)}) %collective-permute-start) | collective-permute-done | bytes 139296 | tf_op jit(solution)/shard_map/ppermute | solution.py:243
  30.3 3.7 %collective-permute-done.2 = bf16[272,256]{1,0:T(8,128)(2,1)S(1)} collective-permute-done((bf16[272,256]{1,0:T(8,128)(2,1)S(1)}, bf16[272,256]{1,0:T(8,128)(2,1)S(1)}, u32[]{:S(2)}, u32[]{:S(2)}) %collective-permute-start.2) | collective-permute-done | bytes 139296 | tf_op jit(solution)/shard_map/ppermute | solution.py:243
  34.1 13.4 %all-to-all-done = bf16[16,4,32,256]{3,2,1,0:T(8,128)(2,1)S(1)} async-done(((bf16[16,4,32,256]{3,2,1,0:T(8,128)(2,1)}), bf16[16,4,32,256]{3,2,1,0:T(8,128)(2,1)S(1)}, u32[]{:S(2)}, u32[]{:S(2)}) %all-to-all-start) | async-done | bytes 1048608 | tf_op jit(solution)/shard_map/all_to_all | solution.py:27
  47.5 8.1 %collective-permute-start.6 = (bf16[4,272,256]{2,1,0:T(8,128)(2,1)S(1)}, bf16[4,272,256]{2,1,0:T(8,128)(2,1)S(1)}, u32[]{:S(2)}, u32[]{:S(2)}) collective-permute-start(bf16[4,272,256]{2,1,0:T(8,128)(2,1)S(1)} %pad_maximum_fusion.rest_4_.rest_5_), channel_id=1, source_target_pairs={{0,1},{1,0},{2,3},{3,2},{4,5},{5,4},{6,7},{7,6},{8,9},{9,8},{10,11... | collective-permute-start | bytes 1671176 | tf_op jit(solution)/shard_map/ppermute | solution.py:252
  55.7 3.7 %collective-permute-start.5 = (bf16[2,4,4,32,256]{4,3,2,1,0:T(8,128)(2,1)S(1)}, bf16[2,4,4,32,256]{4,3,2,1,0:T(8,128)(2,1)S(1)}, u32[]{:S(2)}, u32[]{:S(2)}) collective-permute-start(bf16[2,4,4,32,256]{4,3,2,1,0:T(8,128)(2,1)S(1)} %get-tuple-element.38), channel_id=1, source_target_pairs={{0,448},{64,0},{128,64},{192,128},{256,192},{320,256},{384,320},{4... | collective-permute-start | bytes 1572872 | tf_op jit(solution)/shard_map/ppermute | solution.py:250
  59.5 2.1 %collective-permute-start.4 = (bf16[2,4,4,32,256]{4,3,2,1,0:T(8,128)(2,1)S(1)}, bf16[2,4,4,32,256]{4,3,2,1,0:T(8,128)(2,1)S(1)}, u32[]{:S(2)}, u32[]{:S(2)}) collective-permute-start(bf16[2,4,4,32,256]{4,3,2,1,0:T(8,128)(2,1)S(1)} %get-tuple-element.39), channel_id=1, source_target_pairs={{0,64},{64,128},{128,192},{192,256},{256,320},{320,384},{384,448},... | collective-permute-start | bytes 1572872 | tf_op jit(solution)/shard_map/ppermute | solution.py:249
  61.6 1.9 %collective-permute-start.3 = (bf16[4,4,4,32,256]{4,3,2,1,0:T(8,128)(2,1)S(1)}, bf16[4,4,4,32,256]{4,3,2,1,0:T(8,128)(2,1)S(1)}, u32[]{:S(2)}, u32[]{:S(2)}) collective-permute-start(bf16[4,4,4,32,256]{4,3,2,1,0:T(8,128)(2,1)S(1)} %bitcast.12), channel_id=1, source_target_pairs={{0,8},{8,0},{1,9},{9,1},{2,10},{10,2},{3,11},{11,3},{4,12},{12,4},... | collective-permute-start | bytes 3145736 | tf_op jit(solution)/shard_map/ppermute | solution.py:251
  63.5 6.8 %collective-permute-done.5 = bf16[2,4,4,32,256]{4,3,2,1,0:T(8,128)(2,1)S(1)} collective-permute-done((bf16[2,4,4,32,256]{4,3,2,1,0:T(8,128)(2,1)S(1)}, bf16[2,4,4,32,256]{4,3,2,1,0:T(8,128)(2,1)S(1)}, u32[]{:S(2)}, u32[]{:S(2)}) %collective-permute-start.5) | collective-permute-done | bytes 524320 | tf_op jit(solution)/shard_map/ppermute | solution.py:250
  70.3 3.1 %collective-permute-done.4 = bf16[2,4,4,32,256]{4,3,2,1,0:T(8,128)(2,1)S(1)} collective-permute-done((bf16[2,4,4,32,256]{4,3,2,1,0:T(8,128)(2,1)S(1)}, bf16[2,4,4,32,256]{4,3,2,1,0:T(8,128)(2,1)S(1)}, u32[]{:S(2)}, u32[]{:S(2)}) %collective-permute-start.4) | collective-permute-done | bytes 524320 | tf_op jit(solution)/shard_map/ppermute | solution.py:249
  73.5 1.9 %collective-permute-start.7 = (bf16[4,4,4,32,256]{4,3,2,1,0:T(8,128)(2,1)S(1)}, bf16[4,4,4,32,256]{4,3,2,1,0:T(8,128)(2,1)S(1)}, u32[]{:S(2)}, u32[]{:S(2)}) collective-permute-start(bf16[4,4,4,32,256]{4,3,2,1,0:T(8,128)(2,1)S(1)} %constant_dynamic-update-slice_fusion.rest_2_), channel_id=1, source_target_pairs={{0,8},{8,0},{1,9},{9,1},{2,10},{10,2},{3,11},{11,3},{4,12},{12,4},... | collective-permute-start | bytes 3145736 | tf_op jit(solution)/shard_map/ppermute | solution.py:255
  75.5 2.6 %collective-permute-done.7.rest_3_ = bf16[4,4,4,32,256]{4,3,2,1,0:T(8,128)(2,1)S(1)} collective-permute-done((bf16[4,4,4,32,256]{4,3,2,1,0:T(8,128)(2,1)S(1)}, bf16[4,4,4,32,256]{4,3,2,1,0:T(8,128)(2,1)S(1)}, u32[]{:S(2)}, u32[]{:S(2)}) %collective-permute-start.7) | collective-permute-done | bytes 1048608 | tf_op jit(solution)/shard_map/ppermute | solution.py:255
  78.1 3.9 %attention.2 = (bf16[256,256]{1,0:T(8,128)(2,1)S(1)}, bf16[2,2,256,256]{3,2,1,0:T(8,128)(2,1)}) custom-call(s32[3]{0:T(128)S(1)} %pad_add_fusion.info, s32[2]{0:T(128)S(1)} %get-tuple-element.20.starts, s32[2]{0:T(128)S(1)} %get-tuple-element.21.stops, f32[8,256]{1,0:T(8,128)S(1)} %fusion.7.params, bf16[2,2,1024,256]{3,2,1,0:T(8,128)(2,1)S(1)} %copy-done, ...), custom_call_target="tpu_custom_call" | custom-call | flops 1107296256 | bytes 6291456 | tf_op jit(solution)/shard_map/attention/pallas_call | solution.py:132
  82.1 20.4 %all_to_all.25.att = bf16[8,256,256]{2,1,0:T(8,128)(2,1)S(1)} all-to-all(bf16[8,256,256]{2,1,0:T(8,128)(2,1)S(1)} %broadcast_in_dim.57), channel_id=1, replica_groups=mesh['zh'=4,'zl'=2,'yh'=4,'c'=2,'x'=4,'yl'=2] {'x','yl'}, dimensions={0} | all-to-all | bytes 2097152 | tf_op jit(solution)/shard_map/all_to_all | solution.py:27
  102.4 1.0 project.2
  103.5 17.7 %all_to_all.26.rest_4_ = bf16[8,256,256]{2,1,0:T(8,128)(2,1)S(1)} all-to-all(bf16[8,256,256]{2,1,0:T(8,128)(2,1)S(1)} %broadcast_in_dim.58), channel_id=1, replica_groups=mesh['zh'=4,'zl'=2,'yh'=4,'c'=2,'x'=4,'yl'=2] {'x','yl'}, dimensions={0} | all-to-all | bytes 2097152 | tf_op jit(solution)/shard_map/all_to_all | solution.py:27
  121.3 4.9 %attention.3 = (bf16[256,256]{1,0:T(8,128)(2,1)S(1)}, bf16[2,2,256,256]{3,2,1,0:T(8,128)(2,1)}, bf16[256,256]{1,0:T(8,128)(2,1)S(1)}) custom-call(s32[3]{0:T(128)S(1)} %pad_add_fusion.info, s32[2]{0:T(128)S(1)} %get-tuple-element.20.starts, s32[2]{0:T(128)S(1)} %get-tuple-element.21.stops, ...), custom_call_target="tpu_custom_call", output_to_operand_aliasing={{1}: (5, {})} | custom-call | flops 1107296256 | bytes 6291456 | tf_op jit(solution)/shard_map/attention/pallas_call | solution.py:132
  126.2 16.9 %all_to_all.27.att = bf16[8,256,256]{2,1,0:T(8,128)(2,1)S(1)} all-to-all(bf16[8,256,256]{2,1,0:T(8,128)(2,1)S(1)} %broadcast_in_dim.59), channel_id=1, replica_groups=mesh['zh'=4,'zl'=2,'yh'=4,'c'=2,'x'=4,'yl'=2] {'x','yl'}, dimensions={0} | all-to-all | bytes 2097152 | tf_op jit(solution)/shard_map/all_to_all | solution.py:27
  143.1 1.2 project.3
  144.3 8.9 %all_to_all.28.stats = f32[8,8,256]{2,1,0:T(8,128)S(1)} all-to-all(f32[8,8,256]{2,1,0:T(8,128)S(1)} %broadcast_in_dim.60), channel_id=1, replica_groups=mesh['zh'=4,'zl'=2,'yh'=4,'c'=2,'x'=4,'yl'=2] {'x','yl'}, dimensions={0} | all-to-all | bytes 131072 | tf_op jit(solution)/shard_map/all_to_all | solution.py:27
  (40 shorter events, 2.7 us)
Async XLA Ops:
  0.6 17.6 %copy-start.5 = (bf16[256]{0:T(256)(128)(2,1)S(1)}, bf16[256]{0:T(256)(128)(2,1)}, u32[]{:S(2)}) copy-start(bf16[256]{0:T(256)(128)(2,1)} %param.18) | copy-start | bytes 1540
  0.6 17.6 %copy-start.6 = (bf16[256]{0:T(256)(128)(2,1)S(1)}, bf16[256]{0:T(256)(128)(2,1)}, u32[]{:S(2)}) copy-start(bf16[256]{0:T(256)(128)(2,1)} %param.19) | copy-start | bytes 1540
  0.7 17.7 %copy-start.1 = (bf16[256,256]{1,0:T(8,128)(2,1)S(1)}, bf16[256,256]{1,0:T(8,128)(2,1)}, u32[]{:S(2)}) copy-start(bf16[256,256]{1,0:T(8,128)(2,1)} %res_ref.1) | copy-start | bytes 393220
  0.7 27.7 %copy-start.4 = (s32[2]{0:T(128)S(1)}, s32[2]{0:T(128)}, u32[]{:S(2)}) copy-start(s32[2]{0:T(128)} %param.12) | copy-start | bytes 28
  0.7 27.7 %copy-start.3 = (s32[2]{0:T(128)S(1)}, s32[2]{0:T(128)}, u32[]{:S(2)}) copy-start(s32[2]{0:T(128)} %param.11) | copy-start | bytes 28
  0.7 27.9 %copy-start.7 = (bf16[256]{0:T(256)(128)(2,1)S(1)}, bf16[256]{0:T(256)(128)(2,1)}, u32[]{:S(2)}) copy-start(bf16[256]{0:T(256)(128)(2,1)} %param.17) | copy-start | bytes 1540
  0.7 27.9 %copy-start.2 = (bf16[3,256]{1,0:T(4,128)(2,1)S(1)}, bf16[3,256]{1,0:T(4,128)(2,1)}, u32[]{:S(2)}) copy-start(bf16[3,256]{1,0:T(4,128)(2,1)} %param.15) | copy-start | bytes 4612
  2.7 44.8 %all-to-all-start = ((bf16[16,4,32,256]{3,2,1,0:T(8,128)(2,1)}), bf16[16,4,32,256]{3,2,1,0:T(8,128)(2,1)S(1)}, u32[]{:S(2)}, u32[]{:S(2)}) async-start(bf16[16,4,32,256]{3,2,1,0:T(8,128)(2,1)} %broadcast_in_dim.23), calls=%async_computation | async-start | bytes 2097152 | tf_op jit(solution)/shard_map/all_to_all | solution.py:27
  18.4 10.2 %collective-permute-start.1 = (bf16[272,256]{1,0:T(8,128)(2,1)S(1)}, bf16[272,256]{1,0:T(8,128)(2,1)S(1)}, u32[]{:S(2)}, u32[]{:S(2)}) collective-permute-start(bf16[272,256]{1,0:T(8,128)(2,1)S(1)} %maximum_maximum_fusion), channel_id=1, source_target_pairs={{0,4},{2,6},{4,0},{6,2},{1,5},{3,7},{5,1},{7,3},{8,12},{10,14},{12... | collective-permute-start | bytes 417800 | tf_op jit(solution)/shard_map/ppermute | solution.py:243
  23.4 6.9 %collective-permute-start = (bf16[272,256]{1,0:T(8,128)(2,1)S(1)}, bf16[272,256]{1,0:T(8,128)(2,1)S(1)}, u32[]{:S(2)}, u32[]{:S(2)}) collective-permute-start(bf16[272,256]{1,0:T(8,128)(2,1)S(1)} %maximum_maximum_fusion), channel_id=1, source_target_pairs={{0,2},{2,0},{4,6},{6,4},{1,3},{3,1},{5,7},{7,5},{8,10},{10,8},{12,... | collective-permute-start | bytes 417800 | tf_op jit(solution)/shard_map/ppermute | solution.py:243
  25.9 8.2 %collective-permute-start.2 = (bf16[272,256]{1,0:T(8,128)(2,1)S(1)}, bf16[272,256]{1,0:T(8,128)(2,1)S(1)}, u32[]{:S(2)}, u32[]{:S(2)}) collective-permute-start(bf16[272,256]{1,0:T(8,128)(2,1)S(1)} %maximum_maximum_fusion), channel_id=1, source_target_pairs={{0,6},{2,4},{4,2},{6,0},{1,7},{3,5},{5,3},{7,1},{8,14},{10,12},{12... | collective-permute-start | bytes 417800 | tf_op jit(solution)/shard_map/ppermute | solution.py:243
  47.5 30.6 %copy-start = (bf16[2,2,1024,256]{3,2,1,0:T(8,128)(2,1)S(1)}, bf16[2,2,1024,256]{3,2,1,0:T(8,128)(2,1)}, u32[]{:S(2)}) copy-start(bf16[2,2,1024,256]{3,2,1,0:T(8,128)(2,1)} %cache_ref.3) | copy-start | bytes 6291460
  47.5 25.9 %collective-permute-start.6 = (bf16[4,272,256]{2,1,0:T(8,128)(2,1)S(1)}, bf16[4,272,256]{2,1,0:T(8,128)(2,1)S(1)}, u32[]{:S(2)}, u32[]{:S(2)}) collective-permute-start(bf16[4,272,256]{2,1,0:T(8,128)(2,1)S(1)} %pad_maximum_fusion.rest_4_.rest_5_), channel_id=1, source_target_pairs={{0,1},{1,0},{2,3},{3,2},{4,5},{5,4},{6,7},{7,6},{8,9},{9,8},{10,11... | collective-permute-start | bytes 1671176 | tf_op jit(solution)/shard_map/ppermute | solution.py:252
  55.7 14.6 %collective-permute-start.5 = (bf16[2,4,4,32,256]{4,3,2,1,0:T(8,128)(2,1)S(1)}, bf16[2,4,4,32,256]{4,3,2,1,0:T(8,128)(2,1)S(1)}, u32[]{:S(2)}, u32[]{:S(2)}) collective-permute-start(bf16[2,4,4,32,256]{4,3,2,1,0:T(8,128)(2,1)S(1)} %get-tuple-element.38), channel_id=1, source_target_pairs={{0,448},{64,0},{128,64},{192,128},{256,192},{320,256},{384,320},{4... | collective-permute-start | bytes 1572872 | tf_op jit(solution)/shard_map/ppermute | solution.py:250
  59.5 14.0 %collective-permute-start.4 = (bf16[2,4,4,32,256]{4,3,2,1,0:T(8,128)(2,1)S(1)}, bf16[2,4,4,32,256]{4,3,2,1,0:T(8,128)(2,1)S(1)}, u32[]{:S(2)}, u32[]{:S(2)}) collective-permute-start(bf16[2,4,4,32,256]{4,3,2,1,0:T(8,128)(2,1)S(1)} %get-tuple-element.39), channel_id=1, source_target_pairs={{0,64},{64,128},{128,192},{192,256},{256,320},{320,384},{384,448},... | collective-permute-start | bytes 1572872 | tf_op jit(solution)/shard_map/ppermute | solution.py:249
  61.6 13.9 %collective-permute-start.3 = (bf16[4,4,4,32,256]{4,3,2,1,0:T(8,128)(2,1)S(1)}, bf16[4,4,4,32,256]{4,3,2,1,0:T(8,128)(2,1)S(1)}, u32[]{:S(2)}, u32[]{:S(2)}) collective-permute-start(bf16[4,4,4,32,256]{4,3,2,1,0:T(8,128)(2,1)S(1)} %bitcast.12), channel_id=1, source_target_pairs={{0,8},{8,0},{1,9},{9,1},{2,10},{10,2},{3,11},{11,3},{4,12},{12,4},... | collective-permute-start | bytes 3145736 | tf_op jit(solution)/shard_map/ppermute | solution.py:251
  73.5 4.6 %collective-permute-start.7 = (bf16[4,4,4,32,256]{4,3,2,1,0:T(8,128)(2,1)S(1)}, bf16[4,4,4,32,256]{4,3,2,1,0:T(8,128)(2,1)S(1)}, u32[]{:S(2)}, u32[]{:S(2)}) collective-permute-start(bf16[4,4,4,32,256]{4,3,2,1,0:T(8,128)(2,1)S(1)} %constant_dynamic-update-slice_fusion.rest_2_), channel_id=1, source_target_pairs={{0,8},{8,0},{1,9},{9,1},{2,10},{10,2},{3,11},{11,3},{4,12},{12,4},... | collective-permute-start | bytes 3145736 | tf_op jit(solution)/shard_map/ppermute | solution.py:255
